TPU v7x, 128 devices: a whole 4x4x4 slice. The times are simulated.
128 devices in a mesh: rows: 32 (over z, y, x_hi), feat: 4 (over x_lo, core).
Axes of the slice: x: 4 (x_hi: 2, x_lo: 2; x = x_hi * 2 + x_lo), y: 4, z: 4, core: 2. Of those that a mesh axis runs over, the one named last changes fastest.
Arguments:
- slab: bfloat16 [98304, 4096], P('rows', 'feat'), may hold values from -12 to 12
- basis: float32 [4096, 256], P('feat'), may hold values from -1 to 1
- cluster_ids: int32 [98304, 1], P('rows'), may hold values from 0 to 63; in each aligned block of 3072 rows (0 to 3071, 3072 to 6143, ...) at most 128 rows name the same one
- kept: int32 [1], replicated, may hold values from 128 to 256
Outputs:
- packed: bfloat16 [64, 4096, 256], P('rows', None, 'feat')
Inputs may be any that keep to these rules, and one draw needn't show every extreme that they name: `cluster_ids`: within the rows of one device (aligned blocks of 3072 rows), no cluster is named by more than 128 rows, a bound that some block reaches.
All inputs are finite; a program needn't handle non-finite values.
Results may differ from a plain program's by a relative error of at most 0.0065.
Values may be sent and summed in bfloat16 or wider, within the bound.
A program may use at most 64 MiB of HBM per device.

v0:
```python
import jax
import jax.numpy as jnp
from jax import lax
from jax.sharding import Mesh
from jax.sharding import PartitionSpec as P

ITERS = 2
CAP = 128
CLUSTERS = 64
FEAT = ("feat_0", "feat_1")


def in_blocks(shard, dim, devices):
    before, after = (shard.shape[:dim], shard.shape[dim + 1 :])
    return jnp.moveaxis(shard.reshape(*before, devices, -1, *after), dim, 0)


def sum_at_owner(shard, axis, dim):
    blocks = in_blocks(shard, dim, lax.axis_size(axis))
    arrived = lax.all_to_all(blocks, axis, split_axis=0, concat_axis=0, tiled=True)
    return arrived.sum(axis=0)


def summed_rows(shard, axes, dim):
    far, near = axes
    own = sum_at_owner(in_blocks(shard, dim, lax.axis_size(far)), near, dim + 1)
    return jnp.sum(lax.all_to_all(own, far, 0, 0, tiled=True), axis=0)


def sent_to_all(shard, axis):
    devices = lax.axis_size(axis)
    return lax.all_to_all(
        jnp.broadcast_to(shard[None], (devices, *shard.shape)), axis, 0, 0, tiled=True
    )


def in_order(blocks, dim):
    lengths = list(blocks.shape[1:])
    lengths[dim] *= blocks.shape[0]
    return jnp.moveaxis(blocks, 0, dim).reshape(lengths)


def whole_of(shard, axes, dim):
    far, near = axes
    first = sent_to_all(shard, far)
    blocks = jnp.swapaxes(sent_to_all(first, near), 0, 1)
    return in_order(blocks.reshape(-1, *shard.shape), dim)


def padded_to(lines, devices):
    spare = -len(lines) % devices
    return jnp.pad(lines, [(0, spare)] + [(0, 0)] * (lines.ndim - 1))


def gathered_copies(shard, axis, dim):
    return in_order(sent_to_all(shard, axis), dim)


def sum_by_parts(shard, axes):
    lines = shard.reshape(-1, shard.shape[-1])
    own = sum_at_owner(padded_to(lines, lax.axis_size(axes)), axes, 0)
    whole = gathered_copies(own, axes, 0)
    return whole[: len(lines)].reshape(shard.shape)


def taken_together(shard, axis):
    everything = sent_to_all(shard, axis)
    return jnp.sum(everything, axis=0)


def inverse_factor(gram):
    lower = jnp.linalg.cholesky(gram)
    eye = jnp.eye(gram.shape[0], dtype=gram.dtype)
    return lax.linalg.triangular_solve(lower, eye, left_side=True, lower=True)


def shards(slab, basis, cluster_ids, kept):
    width = basis.shape[1]
    basis_b = basis.astype(jnp.bfloat16)
    for step in range(ITERS):
        partial_scores = jnp.dot(slab, basis_b, preferred_element_type=jnp.float32)
        score_part = summed_rows(partial_scores, ("feat_0", "feat_1"), 0).astype(jnp.bfloat16)
        scores = whole_of(score_part, ("feat_0", "feat_1"), 0)
        partial_cov = lax.dot_general(
            slab, scores, (((0,), (0,)), ((), ())), preferred_element_type=jnp.float32
        )
        product = sum_by_parts(partial_cov, "rows")
        gram = taken_together(jnp.dot(product.T, product, precision=lax.Precision.HIGHEST), FEAT)
        inverse = inverse_factor(gram)
        basis_b = jnp.dot(product, inverse.T, precision=lax.Precision.HIGHEST).astype(jnp.bfloat16)
    columns = jnp.arange(width, dtype=jnp.int32)
    masked = jnp.where(columns[None, :] < kept[0], basis_b, jnp.zeros((), jnp.bfloat16))
    partial_proj = jnp.dot(slab, masked, preferred_element_type=jnp.float32)
    projected = summed_rows(partial_proj, ("feat_0", "feat_1"), 1).astype(jnp.bfloat16)
    ids = cluster_ids[:, 0]
    onehot = (ids[:, None] == jnp.arange(CLUSTERS, dtype=jnp.int32)[None, :]).astype(jnp.int32)
    running = jnp.cumsum(onehot, axis=0)
    slot = jnp.sum(onehot * running, axis=1) - 1
    flat = ids * CAP + slot
    buffer = jnp.zeros((CLUSTERS * CAP, projected.shape[1]), jnp.bfloat16).at[flat].set(projected)
    buffer = buffer.reshape(CLUSTERS, CAP, projected.shape[1])
    return lax.all_to_all(buffer, "rows", split_axis=0, concat_axis=1, tiled=True)


def solution(mesh):
    torus = Mesh(mesh.devices.reshape(mesh.shape["rows"], 2, 2), ("rows", "feat_0", "feat_1"))
    placed = (P("rows", FEAT), P(FEAT, None), P("rows", None), P())
    return jax.shard_map(
        shards, mesh=torus, in_specs=placed, out_specs=P("rows", None, FEAT), check_vma=False
    )
```

profile of v0, /device:TPU:0, one launch (start us, length us, event | category | flops | bytes accessed | tf_op | source)
XLA Modules:
  0.0 490.6 jit_solution(8780002311730909088)
XLA Ops:
  0.0 5.0 %fusion.6 = f32[3072,256]{1,0:T(8,128)S(1)} fusion(bf16[3072,1024]{1,0:T(8,128)(2,1)} %param.7, f32[1024,256]{1,0:T(8,128)} %param.8), kind=kOutput, calls=%fused_computation.28 | convolution fusion | flops 1610874880 | bytes 10485760 | tf_op jit(solution)/shard_map/dot_general | solution.py:81
  5.0 1.9 copy.114
  6.8 3.9 all-to-all-start
  10.8 3.6 all-to-all-done
  14.4 1.5 reduce_sum.100
  15.9 25.1 %all_to_all.107 = f32[2,768,256]{2,1,0:T(8,128)} all-to-all(f32[2,768,256]{2,1,0:T(8,128)} %reduce_sum.100), channel_id=1, replica_groups=mesh['rows'=32,'feat_0'=2,'feat_1'=2] {'feat_0'}, dimensions={0} | all-to-all | bytes 3145728 | tf_op jit(solution)/shard_map/all_to_all | solution.py:27
  41.0 1.7 reduce_sum.101
  42.8 12.9 %all_to_all.98 = bf16[2,768,256]{2,1,0:T(8,128)(2,1)S(1)} all-to-all(bf16[2,768,256]{2,1,0:T(8,128)(2,1)S(1)} %broadcast_in_dim.29), channel_id=1, replica_groups=mesh['rows'=32,'feat_0'=2,'feat_1'=2] {'feat_0'}, dimensions={0} | all-to-all | bytes 1572864 | tf_op jit(solution)/shard_map/all_to_all | solution.py:32
  55.8 5.3 %all_to_all.99 = bf16[2,2,768,256]{3,2,1,0:T(8,128)(2,1)S(1)} all-to-all(bf16[2,2,768,256]{3,2,1,0:T(8,128)(2,1)S(1)} %broadcast_in_dim.30), channel_id=1, replica_groups=mesh['rows'=32,'feat_0'=2,'feat_1'=2] {'feat_1'}, dimensions={0} | all-to-all | bytes 3145728 | tf_op jit(solution)/shard_map/all_to_all | solution.py:32
  61.2 1.8 convolution_bitcast_fusion.2
  63.4 30.3 %all_to_all.108 = f32[32,32,256]{2,1,0:T(8,128)S(1)} all-to-all(f32[32,32,256]{2,1,0:T(8,128)S(1)} %bitcast.156), channel_id=1, replica_groups=mesh['rows'=32,'feat_0'=2,'feat_1'=2] {'rows'}, dimensions={0} | all-to-all | bytes 2097152 | tf_op jit(solution)/shard_map/all_to_all | solution.py:20
  93.9 21.7 %all_to_all.100 = f32[32,32,256]{2,1,0:T(8,128)S(1)} all-to-all(f32[32,32,256]{2,1,0:T(8,128)S(1)} %broadcast_in_dim.31), channel_id=1, replica_groups=mesh['rows'=32,'feat_0'=2,'feat_1'=2] {'rows'}, dimensions={0} | all-to-all | bytes 2097152 | tf_op jit(solution)/shard_map/all_to_all | solution.py:32
  115.6 1.8 convolution_bitcast_fusion.4
  117.5 1.1 broadcast_in_dim.32
  118.5 3.7 all-to-all-start.6
  122.3 14.3 %all-to-all-done.6 = f32[4,256,256]{2,1,0:T(8,128)S(1)} async-done(((f32[4,256,256]{2,1,0:T(8,128)}), f32[4,256,256]{2,1,0:T(8,128)S(1)}, u32[]{:S(2)}, u32[]{:S(2)}) %all-to-all-start.6) | async-done | bytes 1048608 | tf_op jit(solution)/shard_map/all_to_all | solution.py:32
  136.9 11.7 %cholesky.130 = f32[128,128]{1,0:T(8,128)S(1)} custom-call(f32[128,128]{1,0:T(8,128)S(1)} %cholesky.194), custom_call_target="Cholesky" | custom-call | tf_op jit(solution)/shard_map/jit(cholesky)/cholesky | solution.py:72
  148.7 9.8 %custom-call.13 = f32[1,128,128]{1,2,0:T(8,128)S(1)} custom-call(f32[1,128,128]{2,1,0:T(8,128)S(1)} %get-tuple-element.50), custom_call_target="InvertDiagBlocksLowerTriangular" | custom-call | tf_op jit(solution)/shard_map/jit(cholesky)/cholesky | solution.py:72
  159.0 11.7 %cholesky.147 = f32[128,128]{1,0:T(8,128)S(1)} custom-call(f32[128,128]{1,0:T(8,128)S(1)} %convolution_subtract_fusion.3), custom_call_target="Cholesky" | custom-call | tf_op jit(solution)/shard_map/jit(cholesky)/cholesky | solution.py:72
  170.7 0.6 compare_reduce_fusion.2
  172.7 3.8 while.4
  173.3 1.3 bitcast_dynamic-update-slice_fusion.4
  175.2 1.3 bitcast_dynamic-update-slice_fusion.4
  176.5 20.1 %custom-call.14 = f32[2,128,128]{1,2,0:T(8,128)S(1)} custom-call(f32[2,128,128]{2,1,0:T(8,128)S(1)} %get-tuple-element.21), custom_call_target="InvertDiagBlocksLowerTriangular" | custom-call | tf_op jit(solution)/shard_map/triangular_solve/custom-call.0 | solution.py:74
  197.5 1.0 convolution_convert_fusion.1
  198.6 6.3 %convolution_bitcast_fusion = f32[3072,256]{0,1:T(8,128)} fusion(bf16[1024,256]{1,0:T(8,128)(2,1)S(1)} %convolution_convert_fusion.1, bf16[3072,1024]{1,0:T(8,128)(2,1)} %param.7), kind=kOutput, calls=%fused_computation.5 | convolution fusion | flops 1610612736 | bytes 9961472 | tf_op jit(solution)/shard_map/dot_general | solution.py:81
  204.9 4.2 reshape_reshape.14
  209.1 1.6 copy.113
  210.7 6.4 %all_to_all.101 = f32[2,2,768,256]{2,1,3,0:T(2,128)S(1)} all-to-all(f32[2,2,768,256]{2,1,3,0:T(2,128)S(1)} %bitcast.150), channel_id=1, replica_groups=mesh['rows'=32,'feat_0'=2,'feat_1'=2] {'feat_1'}, dimensions={0} | all-to-all | bytes 6291456 | tf_op jit(solution)/shard_map/all_to_all | solution.py:20
  217.2 3.7 reduce_sum.104
  220.9 1.5 copy.89
  222.4 23.1 %all_to_all.109 = f32[2,768,256]{1,2,0:T(8,128)} all-to-all(f32[2,768,256]{1,2,0:T(8,128)S(1)} %copy.89), channel_id=1, replica_groups=mesh['rows'=32,'feat_0'=2,'feat_1'=2] {'feat_0'}, dimensions={0} | all-to-all | bytes 3145728 | tf_op jit(solution)/shard_map/all_to_all | solution.py:27
  245.5 1.7 reduce_sum.105
  247.4 12.9 %all_to_all.102 = bf16[2,768,256]{2,1,0:T(8,128)(2,1)S(1)} all-to-all(bf16[2,768,256]{2,1,0:T(8,128)(2,1)S(1)} %broadcast_in_dim.33), channel_id=1, replica_groups=mesh['rows'=32,'feat_0'=2,'feat_1'=2] {'feat_0'}, dimensions={0} | all-to-all | bytes 1572864 | tf_op jit(solution)/shard_map/all_to_all | solution.py:32
  260.5 5.3 %all_to_all.103 = bf16[2,2,768,256]{3,2,1,0:T(8,128)(2,1)S(1)} all-to-all(bf16[2,2,768,256]{3,2,1,0:T(8,128)(2,1)S(1)} %broadcast_in_dim.34), channel_id=1, replica_groups=mesh['rows'=32,'feat_0'=2,'feat_1'=2] {'feat_1'}, dimensions={0} | all-to-all | bytes 3145728 | tf_op jit(solution)/shard_map/all_to_all | solution.py:32
  265.9 1.8 convolution_bitcast_fusion.1
  268.1 23.1 %all_to_all.110 = f32[32,32,256]{2,1,0:T(8,128)S(1)} all-to-all(f32[32,32,256]{2,1,0:T(8,128)S(1)} %bitcast.157), channel_id=1, replica_groups=mesh['rows'=32,'feat_0'=2,'feat_1'=2] {'rows'}, dimensions={0} | all-to-all | bytes 2097152 | tf_op jit(solution)/shard_map/all_to_all | solution.py:20
  291.4 21.7 %all_to_all.104 = f32[32,32,256]{2,1,0:T(8,128)S(1)} all-to-all(f32[32,32,256]{2,1,0:T(8,128)S(1)} %broadcast_in_dim.35), channel_id=1, replica_groups=mesh['rows'=32,'feat_0'=2,'feat_1'=2] {'rows'}, dimensions={0} | all-to-all | bytes 2097152 | tf_op jit(solution)/shard_map/all_to_all | solution.py:32
  313.1 1.8 convolution_bitcast_fusion.3
  314.9 1.1 broadcast_in_dim.36
  316.0 3.7 all-to-all-start.13
  320.4 0.9 fusion.5
  321.3 31.9 %reduce-window.6 = s32[64,24,128]{2,1,0:T(8,128)S(1)} reduce-window(s32[64,24,128]{2,1,0:T(8,128)} %fusion.5, s32[]{:T(128)} %copy.147), window={size=1x1x128 pad=0_0x0_0x127_0}, to_apply=%region_0.0 | reduce-window | flops 24969216 | bytes 1572868 | tf_op jit(solution)/shard_map/reduce-window
  353.2 1.1 slice.74
  354.3 1.6 copy.101
  356.8 11.7 %cholesky.164 = f32[128,128]{1,0:T(8,128)S(1)} custom-call(f32[128,128]{1,0:T(8,128)S(1)} %cholesky.197), custom_call_target="Cholesky" | custom-call | tf_op jit(solution)/shard_map/jit(cholesky)/cholesky | solution.py:72
  368.6 9.8 %custom-call.15 = f32[1,128,128]{1,2,0:T(8,128)S(1)} custom-call(f32[1,128,128]{2,1,0:T(8,128)S(1)} %get-tuple-element.46), custom_call_target="InvertDiagBlocksLowerTriangular" | custom-call | tf_op jit(solution)/shard_map/jit(cholesky)/cholesky | solution.py:72
  378.9 11.7 %cholesky.181 = f32[128,128]{1,0:T(8,128)S(1)} custom-call(f32[128,128]{1,0:T(8,128)S(1)} %convolution_subtract_fusion.2), custom_call_target="Cholesky" | custom-call | tf_op jit(solution)/shard_map/jit(cholesky)/cholesky | solution.py:72
  390.7 0.7 compare_reduce_fusion
  391.4 0.6 compare_reduce_fusion.1
  393.4 4.1 while.5
  394.0 1.4 bitcast_dynamic-update-slice_fusion.5
  396.1 1.4 bitcast_dynamic-update-slice_fusion.5
  397.5 19.9 %custom-call.16 = f32[2,128,128]{1,2,0:T(8,128)S(1)} custom-call(f32[2,128,128]{2,1,0:T(8,128)S(1)} %get-tuple-element.22), custom_call_target="InvertDiagBlocksLowerTriangular" | custom-call | tf_op jit(solution)/shard_map/triangular_solve/custom-call.0 | solution.py:74
  418.4 1.0 fusion
  419.4 4.7 fusion.35
  424.5 6.3 %all_to_all.105 = f32[2,2,3072,64]{2,3,1,0:T(8,128)S(1)} all-to-all(f32[2,2,3072,64]{2,3,1,0:T(8,128)S(1)} %copy.95), channel_id=1, replica_groups=mesh['rows'=32,'feat_0'=2,'feat_1'=2] {'feat_1'}, dimensions={0} | all-to-all | bytes 6291456 | tf_op jit(solution)/shard_map/all_to_all | solution.py:20
  430.7 1.5 reduce_sum.108
  432.2 3.7 all-to-all-start.15
  435.9 20.0 %all-to-all-done.15 = f32[2,3072,64]{1,2,0:T(8,128)S(1)} async-done(((f32[2,3072,64]{1,2,0:T(8,128)}), f32[2,3072,64]{1,2,0:T(8,128)S(1)}, u32[]{:S(2)}, u32[]{:S(2)}) %all-to-all-start.15) | async-done | bytes 1572896 | tf_op jit(solution)/shard_map/all_to_all | solution.py:27
  456.4 9.0 %scatter_custom_fusion = bf16[8192,64]{1,0:T(8,128)(2,1)S(1)} fusion(s32[3072]{0:T(1024)S(1)} %bitcast.167, bf16[3072,64]{1,0:T(8,128)(2,1)S(1)} %copy.97, bf16[]{:T(256)} %constant.68.clone.1), kind=kCustom, calls=%fused_computation.20 | custom fusion | bytes 1048578 | tf_op jit(solution)/shard_map/scatter | solution.py:100
  465.4 0.9 copy.99
  466.4 22.5 %all_to_all.106 = bf16[64,128,64]{1,2,0:T(8,128)(2,1)S(1)} all-to-all(bf16[64,128,64]{1,2,0:T(8,128)(2,1)S(1)} %copy.99), channel_id=1, replica_groups=mesh['rows'=32,'feat_0'=2,'feat_1'=2] {'rows'}, dimensions={0} | all-to-all | bytes 2097152 | tf_op jit(solution)/shard_map/all_to_all | solution.py:102
  488.9 1.2 copy.115
  (74 shorter events, 9.1 us)
Async XLA Ops:
  6.8 7.6 %all-to-all-start = ((f32[2,2,768,256]{3,2,1,0:T(8,128)}), f32[2,2,768,256]{3,2,1,0:T(8,128)S(1)}, u32[]{:S(2)}, u32[]{:S(2)}) async-start(f32[2,2,768,256]{3,2,1,0:T(8,128)} %bitcast.149), calls=%async_computation | async-start | bytes 6291456 | tf_op jit(solution)/shard_map/all_to_all | solution.py:20
  41.0 20.2 %slice-start = ((s8[6291456]{0:T(1024)(128)(4,1)}), s8[2097152]{0:T(1024)(128)(4,1)S(1)}, s32[]{:S(2)}) async-start(s8[6291456]{0:T(1024)(128)(4,1)} %bitcast.145), calls=%async_computation.17 | async-start | bytes 4194304
  55.7 5.5 %slice-start.1 = ((s8[6291456]{0:T(1024)(128)(4,1)}), s8[4194304]{0:T(1024)(128)(4,1)S(1)}, s32[]{:S(2)}) async-start(s8[6291456]{0:T(1024)(128)(4,1)} %bitcast.145), calls=%async_computation.18 | async-start | bytes 8388608
  118.5 18.1 %all-to-all-start.6 = ((f32[4,256,256]{2,1,0:T(8,128)}), f32[4,256,256]{2,1,0:T(8,128)S(1)}, u32[]{:S(2)}, u32[]{:S(2)}) async-start(f32[4,256,256]{2,1,0:T(8,128)} %broadcast_in_dim.32), calls=%async_computation.6 | async-start | bytes 2097152 | tf_op jit(solution)/shard_map/all_to_all | solution.py:32
  245.5 20.3 %slice-start.2 = ((s8[6291456]{0:T(1024)(128)(4,1)}), s8[2097152]{0:T(1024)(128)(4,1)S(1)}, s32[]{:S(2)}) async-start(s8[6291456]{0:T(1024)(128)(4,1)} %bitcast.147), calls=%async_computation.19 | async-start | bytes 4194304
  260.4 5.5 %slice-start.3 = ((s8[6291456]{0:T(1024)(128)(4,1)}), s8[4194304]{0:T(1024)(128)(4,1)S(1)}, s32[]{:S(2)}) async-start(s8[6291456]{0:T(1024)(128)(4,1)} %bitcast.147), calls=%async_computation.20 | async-start | bytes 8388608
  313.1 7.3 %copy-start = (s32[3072,1]{0,1:T(1,128)S(1)}, s32[3072,1]{0,1:T(1,128)}, u32[]{:S(2)}) copy-start(s32[3072,1]{0,1:T(1,128)} %param.9) | copy-start | bytes 36868
  316.0 40.6 %all-to-all-start.13 = ((f32[4,256,256]{2,1,0:T(8,128)}), f32[4,256,256]{2,1,0:T(8,128)S(1)}, u32[]{:S(2)}, u32[]{:S(2)}) async-start(f32[4,256,256]{2,1,0:T(8,128)} %broadcast_in_dim.36), calls=%async_computation.13 | async-start | bytes 2097152 | tf_op jit(solution)/shard_map/all_to_all | solution.py:32
  432.2 23.7 %all-to-all-start.15 = ((f32[2,3072,64]{1,2,0:T(8,128)}), f32[2,3072,64]{1,2,0:T(8,128)S(1)}, u32[]{:S(2)}, u32[]{:S(2)}) async-start(f32[2,3072,64]{1,2,0:T(8,128)} %reduce_sum.108), calls=%async_computation.15 | async-start | bytes 3145728 | tf_op jit(solution)/shard_map/all_to_all | solution.py:27
where the time goes:
time: 500 us; the launch traced here: 491 us
  blocking collectives  217 us (43%)
  other arithmetic  153 us (31%)
  waiting for transfers between devices  37.9 us (8%)
  local copies, waits for them, and re-layouts  35.8 us (7%)
  matrix products  28 us (6%)
  starting transfers between devices  15.1 us (3%)
    all_to_all x6, blocking collectives, sent_to_all(): lax.all_to_all(jnp.broadcast_to(shard[None], (devices, *shard.shape)), ax...  79.8 us
    another operation x13, other arithmetic, inverse_factor(): lower = jnp.linalg.cholesky(gram)  68.6 us
    all_to_all x4, blocking collectives, sum_at_owner(): lax.all_to_all(blocks, axis, split_axis=0, concat_axis=0, tiled=True)  66.2 us
    all_to_all x2, blocking collectives, summed_rows(): return jnp.sum(lax.all_to_all(own, far, 0, 0, tiled=True), axis=0)  48.2 us
    another operation x5, other arithmetic, inverse_factor(): return lax.linalg.triangular_solve(lower, eye, left_side=True, lower=True)  40.1 us
    another operation x3, other arithmetic  32.4 us
    all_to_all x1, blocking collectives, shards(): lax.all_to_all(buffer, 'rows', split_axis=0, concat_axis=1, tiled=True)  22.5 us
    all_to_all x1, waiting for transfers between devices, summed_rows(): return jnp.sum(lax.all_to_all(own, far, 0, 0, tiled=True), axis=0)  20 us
  transfers between devices with their start and end apart: 4, of which 3 were waited for; matrix products, arithmetic and copies ran while one was open for 7% of the time, Pallas kernels for 0%

commit v1 on v0

v1 whole, which is shorter than its diff:
```python
import functools

import jax
import jax.numpy as jnp
from jax import lax
from jax.experimental import pallas as pl
from jax.experimental.pallas import tpu as pltpu
from jax.sharding import Mesh
from jax.sharding import PartitionSpec as P

ITERS = 2
CAP = 128
NC = 4
TOL = 2e-3
STEPS = 12
F32 = jnp.float32
BF16 = jnp.bfloat16
MESH = pl.DeviceIdType.MESH
VMEM = pl.BlockSpec(memory_space=pltpu.VMEM)
ANY = pl.BlockSpec(memory_space=pl.ANY)
FEAT = ("xl", "core")


def nn(a, b, precision=None):
    return lax.dot_general(
        a, b, (((1,), (0,)), ((), ())), precision=precision, preferred_element_type=F32
    )


def nt(a, b, precision=None):
    return lax.dot_general(
        a, b, (((1,), (1,)), ((), ())), precision=precision, preferred_element_type=F32
    )


def tn(a, b):
    return lax.dot_general(a, b, (((0,), (0,)), ((), ())), preferred_element_type=F32)


def greet(targets):
    barrier = pltpu.get_barrier_semaphore()
    for target in targets:
        pl.semaphore_signal(barrier, inc=1, device_id=target, device_id_type=MESH)
    return barrier


def greet_rows(barrier, me, count):
    @pl.loop(1, count)
    def _(d):
        peer = lax.rem(me + d, count)
        pl.semaphore_signal(barrier, inc=1, device_id={"rows": peer}, device_id_type=MESH)


def remote(src, dst, send, recv, target):
    return pltpu.make_async_remote_copy(
        src_ref=src, dst_ref=dst, send_sem=send, recv_sem=recv, device_id=target, device_id_type=MESH
    )


def slab_loads(slab, held, sems, core, chunk):
    half = NC * chunk

    def load(own, i):
        h = core if own else 1 - core
        start = pl.multiple_of(h * half + i * chunk, chunk)
        return pltpu.make_async_copy(slab.at[pl.ds(start, chunk)], held.at[h, i], sems.at[int(own), i])

    for i in range(NC):
        load(False, i).start()
        load(True, i).start()
    return load


def covariance_kernel(rows, slab, q, z_out, gram_out, held, away, home, part, mine, theirs, y, z,
                      z_send, z_recv, z_full, g_part, g_near, g_mine, g_far, g_all,
                      load_sem, near_sem, far_sem, y_sem, rs_sem, ag_sem, g_sem):
    me, core, xl = lax.axis_index("rows"), lax.axis_index("core"), lax.axis_index("xl")
    near, far = {"core": 1 - core}, {"xl": 1 - xl}
    chunk = slab.shape[0] // (2 * NC)
    width = q.shape[1]
    barrier = greet((near, far))
    greet_rows(barrier, me, rows)
    load = slab_loads(slab, held, load_sem, core, chunk)

    def to_near(i):
        return remote(away.at[i], home.at[i], near_sem.at[0, i], near_sem.at[1, i], near)

    def to_far(i):
        return remote(mine.at[i], theirs.at[i], far_sem.at[0, i], far_sem.at[1, i], far)

    def share(i):
        return remote(y.at[core, i], y.at[core, i], y_sem.at[0, i], y_sem.at[1, i], near)

    def shared(i):
        return remote(y.at[1 - core, i], y.at[1 - core, i], y_sem.at[0, i], y_sem.at[1, i], near)

    def chip_sum(i):
        to_near(i).wait_recv()
        mine[i] = (part[i] + home[i].astype(F32)).astype(BF16)
        to_far(i).start()

    for i in range(NC):
        load(False, i).wait()
        away[i] = nn(held[1 - core, i], q[...]).astype(BF16)
        if i == 0:
            pl.semaphore_wait(barrier, rows + 1)
        to_near(i).start()
        load(True, i).wait()
        part[i] = nn(held[core, i], q[...])
        if i > 0:
            chip_sum(i - 1)
    chip_sum(NC - 1)

    def add(h, i, first=False):
        term = tn(y[h, i], held[h, i])
        z[...] = term if first else z[...] + term

    for i in range(NC):
        to_far(i).wait_recv()
        y[core, i] = (mine[i].astype(F32) + theirs[i].astype(F32)).astype(BF16)
        share(i).start()
        add(core, i, i == 0)
        if i > 0:
            shared(i - 1).wait_recv()
            add(1 - core, i - 1)
    shared(NC - 1).wait_recv()
    add(1 - core, NC - 1)

    deep, wide = z_send.shape[1:]
    group = rows // 2
    for p in range(rows):
        f, k = divmod(p, group)
        z_send[p] = z[k * deep:(k + 1) * deep, f * wide:(f + 1) * wide].astype(BF16)

    def scatter(d):
        peer = lax.rem(me + d, rows)
        return remote(z_send.at[peer], z_recv.at[d - 1], rs_sem.at[0, d - 1], rs_sem.at[1, d - 1],
                      {"rows": peer})

    def gather(d):
        peer = lax.rem(me + d, rows)
        return remote(z_full.at[me], z_full.at[me], ag_sem.at[0, d - 1], ag_sem.at[1, d - 1],
                      {"rows": peer})

    def gathered(d):
        peer = lax.rem(me - d + rows, rows)
        return remote(z_full.at[peer], z_full.at[peer], ag_sem.at[0, d - 1], ag_sem.at[1, d - 1],
                      {"rows": peer})

    @pl.loop(1, rows)
    def _(d):
        scatter(d).start()

    def total(d, acc):
        scatter(d).wait_recv()
        return acc + z_recv[d - 1].astype(F32)

    z_full[me] = lax.fori_loop(1, rows, total, z_send[me].astype(F32)).astype(BF16)

    @pl.loop(1, rows)
    def _(d):
        gather(d).start()

    @pl.loop(1, rows)
    def _(d):
        gathered(d).wait_recv()

    half = width // 2
    first = z_full[0:group].reshape(width, wide)
    second = z_full[group:rows].reshape(width, wide)
    g_part[...] = (nt(first, first) + nt(second, second)).reshape(2, half, width)
    out_near = remote(g_part.at[1 - core], g_near, g_sem.at[0, 0], g_sem.at[1, 0], near)
    out_far = remote(g_mine, g_far, g_sem.at[0, 1], g_sem.at[1, 1], far)
    out_back = remote(g_all.at[core], g_all.at[core], g_sem.at[0, 2], g_sem.at[1, 2], near)
    in_back = remote(g_all.at[1 - core], g_all.at[1 - core], g_sem.at[0, 2], g_sem.at[1, 2], near)
    out_near.start()
    z_out[...] = z_full[...]
    out_near.wait_recv()
    g_mine[...] = g_part[core] + g_near[...]
    out_far.start()
    out_far.wait_recv()
    g_all[core] = g_mine[...] + g_far[...]
    out_back.start()
    in_back.wait_recv()
    gram_out[...] = g_all[...].reshape(width, width)
    for i in range(NC):
        to_near(i).wait_send()
        to_far(i).wait_send()
        share(i).wait_send()

    @pl.loop(1, rows)
    def _(d):
        scatter(d).wait_send()
        gather(d).wait_send()

    out_near.wait_send()
    out_far.wait_send()
    out_back.wait_send()


def covariance(slab, q, rows, ident):
    length, feats = slab.shape
    width = q.shape[1]
    chunk = length // (2 * NC)
    piece = (2 * width // rows, feats // 2)
    half = (width // 2, width)
    dma = pltpu.SemaphoreType.DMA
    return pl.pallas_call(
        functools.partial(covariance_kernel, rows),
        out_shape=(
            jax.ShapeDtypeStruct((rows, *piece), BF16),
            jax.ShapeDtypeStruct((width, width), F32),
        ),
        in_specs=[ANY, VMEM],
        out_specs=(VMEM, VMEM),
        scratch_shapes=[
            pltpu.VMEM((2, NC, chunk, feats), BF16),
            pltpu.VMEM((NC, chunk, width), BF16),
            pltpu.VMEM((NC, chunk, width), BF16),
            pltpu.VMEM((NC, chunk, width), F32),
            pltpu.VMEM((NC, chunk, width), BF16),
            pltpu.VMEM((NC, chunk, width), BF16),
            pltpu.VMEM((2, NC, chunk, width), BF16),
            pltpu.VMEM((width, feats), F32),
            pltpu.VMEM((rows, *piece), BF16),
            pltpu.VMEM((rows - 1, *piece), BF16),
            pltpu.VMEM((rows, *piece), BF16),
            pltpu.VMEM((2, *half), F32),
            pltpu.VMEM(half, F32),
            pltpu.VMEM(half, F32),
            pltpu.VMEM(half, F32),
            pltpu.VMEM((2, *half), F32),
            dma((2, NC)),
            dma((2, NC)),
            dma((2, NC)),
            dma((2, NC)),
            dma((2, rows - 1)),
            dma((2, rows - 1)),
            dma((2, 3)),
        ],
        compiler_params=pltpu.CompilerParams(
            collective_id=ident, has_side_effects=True, vmem_limit_bytes=48 << 20
        ),
        name="covariance",
    )(slab, q)


def basis_kernel(last, kept, gram, z, q_out, x, e, a, state):
    n = gram.shape[0]
    row = lax.broadcasted_iota(jnp.int32, (n, n), 0)
    col = lax.broadcasted_iota(jnp.int32, (n, n), 1)
    lower = jnp.where(row > col, F32(1), jnp.where(row == col, F32(0.5), F32(0)))
    eye = jnp.where(row == col, F32(1), F32(0))
    high = lax.Precision.HIGHEST

    g = gram[...]
    diag = g * eye
    across = lax.rsqrt(jnp.sum(diag, axis=0, keepdims=True))
    down = lax.rsqrt(jnp.sum(diag, axis=1, keepdims=True))
    e[...] = g * across * down - eye
    x[...] = eye * across
    state[0] = 0
    state[1] = 0

    @pl.loop(0, STEPS)
    def _(step):
        @pl.when(state[0] == 0)
        def _():
            now = e[...]
            err = jnp.sum(now * now)
            x[...] = x[...] - nn(now * lower, x[...], high)
            done = err < TOL * TOL
            state[0] = done.astype(jnp.int32)

            @pl.when(jnp.logical_not(done))
            def _():
                e[...] = nt(nn(x[...], gram[...], high), x[...], high) - eye

    @pl.when(state[0] == 0)
    def _():
        a[...] = gram[...]
        x[...] = eye

        @pl.loop(0, n)
        def _(j):
            pick_row = row == j
            pick_col = col == j
            now = a[...]
            inv = x[...]
            a_row = jnp.sum(jnp.where(pick_row, now, 0.0), axis=0, keepdims=True)
            a_col = jnp.sum(jnp.where(pick_col, now, 0.0), axis=1, keepdims=True)
            x_row = jnp.sum(jnp.where(pick_row, inv, 0.0), axis=0, keepdims=True)
            pivot = jnp.sum(jnp.where(pick_row & pick_col, now, 0.0))
            root = jnp.sqrt(jnp.full((1, n), pivot))
            scaled = x_row / root
            factor = jnp.where(row[:, :1] > j, a_col / root[:, :1], 0.0)
            x[...] = jnp.where(pick_row, scaled, inv - factor * scaled)
            a[...] = now - factor * (a_row / root)

    inverse = x[...]
    top = inverse.astype(BF16)
    rest = (inverse - top.astype(F32)).astype(BF16)
    rows = z.shape[0]
    wide = z.shape[2]
    for f in range(2):
        block = z[f * (rows // 2):(f + 1) * (rows // 2)].reshape(n, wide)
        qt = nn(top, block) + nn(rest, block)
        if last:
            index = lax.broadcasted_iota(jnp.int32, (n, wide), 0)
            qt = jnp.where(index < kept[0], qt, 0.0)
        q_out[f * wide:(f + 1) * wide, :] = qt.T.astype(BF16)


def new_basis(kept, gram, z, last):
    n = gram.shape[0]
    return pl.pallas_call(
        functools.partial(basis_kernel, last),
        out_shape=jax.ShapeDtypeStruct((2 * z.shape[2], n), BF16),
        in_specs=[pl.BlockSpec(memory_space=pltpu.SMEM), VMEM, VMEM],
        out_specs=VMEM,
        scratch_shapes=[
            pltpu.VMEM((n, n), F32),
            pltpu.VMEM((n, n), F32),
            pltpu.VMEM((n, n), F32),
            pltpu.SMEM((2,), jnp.int32),
        ],
        name="new_basis",
    )(kept, gram, z)


def project_kernel(slab, q, p_out, held, away, home, part, keep, send, recv, p,
                   load_sem, near_sem, far_sem, p_sem):
    core, xl = lax.axis_index("core"), lax.axis_index("xl")
    near, far = {"core": 1 - core}, {"xl": 1 - xl}
    chunk = slab.shape[0] // (2 * NC)
    width = q.shape[1]
    half = width // 2
    barrier = greet((near, far))
    load = slab_loads(slab, held, load_sem, core, chunk)

    def to_near(i):
        return remote(away.at[i], home.at[i], near_sem.at[0, i], near_sem.at[1, i], near)

    def to_far(i):
        return remote(send.at[i], recv.at[i], far_sem.at[0, i], far_sem.at[1, i], far)

    def share(i):
        return remote(p.at[core, i], p.at[core, i], p_sem.at[0, i], p_sem.at[1, i], near)

    def shared(i):
        return remote(p.at[1 - core, i], p.at[1 - core, i], p_sem.at[0, i], p_sem.at[1, i], near)

    def chip_sum(i):
        to_near(i).wait_recv()
        both = part[i] + home[i].astype(F32)
        low, high = both[:, :half], both[:, half:]
        keep[i] = jnp.where(xl == 0, low, high)
        send[i] = jnp.where(xl == 0, high, low).astype(BF16)
        to_far(i).start()

    for i in range(NC):
        load(False, i).wait()
        away[i] = nn(held[1 - core, i], q[...]).astype(BF16)
        if i == 0:
            pl.semaphore_wait(barrier, 2)
        to_near(i).start()
        load(True, i).wait()
        part[i] = nn(held[core, i], q[...])
        if i > 0:
            chip_sum(i - 1)
    chip_sum(NC - 1)
    for i in range(NC):
        to_far(i).wait_recv()
        p[core, i] = (keep[i] + recv[i].astype(F32)).astype(BF16)
        share(i).start()
    for i in range(NC):
        shared(i).wait_recv()
    p_out[...] = p[...].reshape(p_out.shape)
    for i in range(NC):
        to_near(i).wait_send()
        to_far(i).wait_send()
        share(i).wait_send()


def project(slab, q, ident):
    length, feats = slab.shape
    width = q.shape[1]
    chunk = length // (2 * NC)
    half = width // 2
    dma = pltpu.SemaphoreType.DMA
    return pl.pallas_call(
        project_kernel,
        out_shape=jax.ShapeDtypeStruct((length, half), BF16),
        in_specs=[ANY, VMEM],
        out_specs=VMEM,
        scratch_shapes=[
            pltpu.VMEM((2, NC, chunk, feats), BF16),
            pltpu.VMEM((NC, chunk, width), BF16),
            pltpu.VMEM((NC, chunk, width), BF16),
            pltpu.VMEM((NC, chunk, width), F32),
            pltpu.VMEM((NC, chunk, half), F32),
            pltpu.VMEM((NC, chunk, half), BF16),
            pltpu.VMEM((NC, chunk, half), BF16),
            pltpu.VMEM((2, NC, chunk, half), BF16),
            dma((2, NC)),
            dma((2, NC)),
            dma((2, NC)),
            dma((2, NC)),
        ],
        compiler_params=pltpu.CompilerParams(
            collective_id=ident, has_side_effects=True, vmem_limit_bytes=40 << 20
        ),
        name="project",
    )(slab, q)


def place_kernel(clusters, ids, place):
    blocks = ids.shape[0]
    lane = lax.broadcasted_iota(jnp.int32, (CAP, CAP), 1)
    sub = lax.broadcasted_iota(jnp.int32, (CAP, CAP), 0)
    before = jnp.where(sub < lane, F32(1), F32(0)).astype(BF16)
    names = lax.broadcasted_iota(jnp.int32, (clusters, CAP), 0)
    seen = jnp.zeros((clusters, 1), F32)
    for b in range(blocks):
        block = ids[b:b + 1, :]
        hot = jnp.where(names == block, F32(1), F32(0))
        earlier = nn(hot.astype(BF16), before) + seen
        slot = jnp.sum(hot * earlier, axis=0, keepdims=True).astype(jnp.int32)
        pair = lax.div(block, 2)
        odd = block - 2 * pair
        place[b:b + 1, :] = odd * (clusters // 2 * CAP) + pair * CAP + slot
        seen = seen + jnp.sum(hot, axis=1, keepdims=True)


def places(cluster_ids, clusters):
    ids = cluster_ids.reshape(-1, CAP)
    return pl.pallas_call(
        functools.partial(place_kernel, clusters),
        out_shape=jax.ShapeDtypeStruct(ids.shape, jnp.int32),
        in_specs=[VMEM],
        out_specs=VMEM,
        name="places",
    )(ids).reshape(-1)


def pack_kernel(place, side, p, out, doubled, spread):
    rows = out.shape[0]
    length, lanes = p.shape
    cols = lanes // 2
    unroll = 16
    low = lax.broadcasted_iota(jnp.int32, (length, lanes), 1) < cols
    wide = p[...].astype(F32)
    turned = pltpu.roll(wide, cols, 1)
    doubled[...] = jnp.where(low == (side[0] == 0), wide, turned)
    spread[...] = jnp.zeros_like(spread)

    @pl.loop(0, length // unroll)
    def _(step):
        for u in range(unroll):
            i = step * unroll + u
            spread[pl.ds(place[i], 1), :] = doubled[pl.ds(i, 1), :]

    even = lax.broadcasted_iota(jnp.int32, (CAP, lanes), 1) < cols

    @pl.loop(0, rows)
    def _(r):
        start = pl.multiple_of(r * CAP, CAP)
        first = spread[pl.ds(start, CAP), :]
        second = spread[pl.ds(pl.multiple_of(rows * CAP + start, CAP), CAP), :]
        out[r] = jnp.where(even, first, second).T.astype(BF16)


def packed_rows(place, side, p, rows):
    length, lanes = p.shape
    smem = pl.BlockSpec(memory_space=pltpu.SMEM)
    return pl.pallas_call(
        pack_kernel,
        out_shape=jax.ShapeDtypeStruct((rows, lanes, CAP), BF16),
        in_specs=[smem, smem, VMEM],
        out_specs=VMEM,
        scratch_shapes=[pltpu.VMEM((length, lanes), F32), pltpu.VMEM((2 * rows * CAP, lanes), F32)],
        compiler_params=pltpu.CompilerParams(vmem_limit_bytes=32 << 20),
        name="packed_rows",
    )(place, side, p)


def exchange_kernel(rows, buf, out, arrived, sem):
    me = lax.axis_index("rows")
    barrier = pltpu.get_barrier_semaphore()
    greet_rows(barrier, me, rows)
    pl.semaphore_wait(barrier, rows - 1)

    def send(d):
        peer = lax.rem(me + d, rows)
        return remote(buf.at[peer], arrived.at[me], sem.at[0, d - 1], sem.at[1, d - 1], {"rows": peer})

    def came(d):
        peer = lax.rem(me - d + rows, rows)
        return remote(buf.at[peer], arrived.at[peer], sem.at[0, d - 1], sem.at[1, d - 1], {"rows": peer})

    @pl.loop(1, rows)
    def _(d):
        send(d).start()

    arrived[me] = buf[me]

    @pl.loop(1, rows)
    def _(d):
        came(d).wait_recv()

    cols = out.shape[1]
    for r in range(rows):
        for h in range(2):
            out[h, :, r * CAP:(r + 1) * CAP] = arrived[r, h * cols:(h + 1) * cols, :]

    @pl.loop(1, rows)
    def _(d):
        send(d).wait_send()


def exchange(buf, ident):
    rows, lanes, _ = buf.shape
    return pl.pallas_call(
        functools.partial(exchange_kernel, rows),
        out_shape=jax.ShapeDtypeStruct((2, lanes // 2, rows * CAP), BF16),
        in_specs=[VMEM],
        out_specs=VMEM,
        scratch_shapes=[pltpu.VMEM(buf.shape, BF16), pltpu.SemaphoreType.DMA((2, rows - 1))],
        compiler_params=pltpu.CompilerParams(collective_id=ident, has_side_effects=True),
        name="exchange",
    )(buf)


def shards(rows, slab, basis, cluster_ids, kept):
    place = places(cluster_ids, 2 * rows)
    side = jnp.broadcast_to(lax.axis_index("core"), (1,)).astype(jnp.int32)
    q = basis.astype(BF16)
    for step in range(ITERS):
        z, gram = covariance(slab, q, rows, step)
        q = new_basis(kept, gram, z, step == ITERS - 1)
    p = project(slab, q, ITERS)
    buf = packed_rows(place, side, p, rows)
    return jnp.swapaxes(exchange(buf, ITERS + 1), 1, 2)


def solution(mesh):
    rows = mesh.shape["rows"]
    torus = Mesh(mesh.devices.reshape(rows, 2, 2), ("rows", "xl", "core"))
    placed = (P("rows", FEAT), P(FEAT, None), P("rows", None), P())
    return jax.shard_map(
        functools.partial(shards, rows), mesh=torus, in_specs=placed,
        out_specs=P("rows", None, FEAT), check_vma=False,
    )
```

time: 500 us -> 191 us (0.38); the launches traced: 491 us -> 190 us
  blocking collectives: 217 us -> 0 us
  Pallas kernels: 0 us -> 177 us
  other arithmetic: 153 us -> 1.28 us
  waiting for transfers between devices: 37.9 us -> 0 us
  matrix products: 28 us -> 0 us
  local copies, waits for them, and re-layouts: 35.8 us -> 11.1 us
  starting transfers between devices: 15.1 us -> 0 us
    all_to_all x13 -> x0, blocking collectives: 217 us -> none  [the longest x6 79.8 us: sent_to_all(): lax.all_to_all(jnp.broadcast_to(shard[None], (devices, *shard.shape)), ax...]
    pallas_call x0 -> x8, Pallas kernels: none -> 177 us  [the longest x2 113 us: covariance(): pl.pallas_call(functools.partial(covariance_kernel, rows), out_shape=(jax...]
    another operation x21 -> x0, other arithmetic: 141 us -> none  [the longest x13 68.6 us: inverse_factor(): lower = jnp.linalg.cholesky(gram)]
    all_to_all x4 -> x0, waiting for transfers between devices: 37.9 us -> none  [the longest x1 20 us: summed_rows(): return jnp.sum(lax.all_to_all(own, far, 0, 0, tiled=True), axis=0)]
    dot_general x9 -> x0, matrix products: 25.3 us -> none  [the longest x2 11.3 us: shards(): partial_scores = jnp.dot(slab, basis_b, preferred_element_type=jnp.float32)]
    another operation x24 -> x0, local copies, waits for them, and re-layouts: 18.4 us -> none  [the longest x15 7.93 us: inverse_factor(): return lax.linalg.triangular_solve(lower, eye, left_side=True, lower=True)]
    all_to_all x4 -> x0, starting transfers between devices: 15.1 us -> none  [the longest x2 7.46 us: sent_to_all(): lax.all_to_all(jnp.broadcast_to(shard[None], (devices, *shard.shape)), ax...]
    unnamed x10 -> x19, local copies, waits for them, and re-layouts: 0.02 us -> 11.1 us
  transfers between devices with their start and end apart: 4 -> 0, of which waited for: 3 -> 0; matrix products, arithmetic and copies ran while one was open for 7% -> 0% of each run, Pallas kernels for 0% -> 0%
where the time goes in v1:
time: 191 us; the launch traced here: 190 us
  Pallas kernels  177 us (93%)
  local copies, waits for them, and re-layouts  11.1 us (6%)
    pallas_call x2, Pallas kernels, covariance(): pl.pallas_call(functools.partial(covariance_kernel, rows), out_shape=(jax...  113 us
    pallas_call x1, Pallas kernels, exchange(): pl.pallas_call(functools.partial(exchange_kernel, rows), out_shape=jax.Sh...  24.3 us
    pallas_call x2, Pallas kernels, new_basis(): pl.pallas_call(functools.partial(basis_kernel, last), out_shape=jax.Shape...  16.2 us
    pallas_call x1, Pallas kernels, project(): pl.pallas_call(project_kernel, out_shape=jax.ShapeDtypeStruct((length, ha...  14.1 us
    unnamed x19, local copies, waits for them, and re-layouts  11.1 us
    pallas_call x1, Pallas kernels, packed_rows(): pl.pallas_call(pack_kernel, out_shape=jax.ShapeDtypeStruct((rows, lanes,...  7.89 us

profile of v1, /device:TPU:0, one launch (start us, length us, event | category | flops | bytes accessed | tf_op | source)
XLA Modules:
  0.0 189.8 jit_solution(64301401276944016)
XLA Ops:
  0.7 1.7 places.1
  2.3 1.3 convert_element_type.3.q
  3.6 58.3 %covariance.2 = (bf16[32,16,512]{2,1,0:T(8,128)(2,1)S(1)}, f32[256,256]{1,0:T(8,128)S(1)}) custom-call(bf16[3072,1024]{1,0:T(8,128)(2,1)} %slab.5, bf16[1024,256]{1,0:T(8,128)(2,1)S(1)} %convert_element_type.3.q), custom_call_target="tpu_custom_call" | custom-call | tf_op jit(solution)/shard_map/covariance/pallas_call | solution.py:208
  61.9 0.0 copy-start.5
  62.0 0.8 copy-done.5
  62.7 0.0 copy-start.7
  62.7 0.7 copy-done.7
  63.4 8.9 %new_basis.2.q = bf16[1024,256]{1,0:T(8,128)(2,1)} custom-call(s32[1]{0:T(128)S(6)} %copy.6.kept, f32[256,256]{1,0:T(8,128)} %copy-done.7, bf16[32,16,512]{2,1,0:T(8,128)(2,1)} %copy-done.5), custom_call_target="tpu_custom_call" | custom-call | tf_op jit(solution)/shard_map/new_basis/pallas_call | solution.py:316
  72.3 0.0 copy-start.2
  72.3 1.0 copy-done.2
  73.4 0.0 copy-start.8
  73.4 54.3 %covariance.3 = (bf16[32,16,512]{2,1,0:T(8,128)(2,1)S(1)}, f32[256,256]{1,0:T(8,128)S(1)}) custom-call(bf16[3072,1024]{1,0:T(8,128)(2,1)} %slab.5, bf16[1024,256]{1,0:T(8,128)(2,1)S(1)} %copy-done.2), custom_call_target="tpu_custom_call" | custom-call | tf_op jit(solution)/shard_map/covariance/pallas_call | solution.py:208
  127.7 0.0 copy-start.4
  127.7 0.8 copy-done.4
  128.5 0.0 copy-start.6
  128.5 0.7 copy-done.6
  129.2 7.3 %new_basis.3.q = bf16[1024,256]{1,0:T(8,128)(2,1)} custom-call(s32[1]{0:T(128)S(6)} %copy.6.kept, f32[256,256]{1,0:T(8,128)} %copy-done.6, bf16[32,16,512]{2,1,0:T(8,128)(2,1)} %copy-done.4), custom_call_target="tpu_custom_call" | custom-call | tf_op jit(solution)/shard_map/new_basis/pallas_call | solution.py:316
  136.5 0.0 copy-start
  136.5 2.8 %copy-done = bf16[3072,1024]{1,0:T(8,128)(2,1)S(1)} copy-done((bf16[3072,1024]{1,0:T(8,128)(2,1)S(1)}, bf16[3072,1024]{1,0:T(8,128)(2,1)}, u32[]{:S(2)}) %copy-start) | copy-done | bytes 6291480
  139.3 0.0 copy-start.3
  139.3 1.0 copy-done.3
  140.3 14.1 %project.1.p = bf16[3072,128]{1,0:T(8,128)(2,1)S(1)} custom-call(bf16[3072,1024]{1,0:T(8,128)(2,1)S(1)} %copy-done, bf16[1024,256]{1,0:T(8,128)(2,1)S(1)} %copy-done.3), custom_call_target="tpu_custom_call" | custom-call | tf_op jit(solution)/shard_map/project/pallas_call | solution.py:391
  154.4 0.0 copy-done.8
  154.4 7.9 %packed_rows.1.buf = bf16[32,128,128]{2,1,0:T(8,128)(2,1)S(1)} custom-call(s32[3072]{0:T(1024)S(1)} %bitcast.4, s32[1]{0:T(128)} %bitcast.2.side, bf16[3072,128]{1,0:T(8,128)(2,1)S(1)} %project.1.p), custom_call_target="tpu_custom_call" | custom-call | tf_op jit(solution)/shard_map/packed_rows/pallas_call | solution.py:476
  162.3 0.0 copy-start.1
  162.3 1.0 copy-done.1
  163.2 24.3 %exchange.1 = bf16[2,64,4096]{2,1,0:T(8,128)(2,1)} custom-call(bf16[32,128,128]{2,1,0:T(8,128)(2,1)} %copy-done.1), custom_call_target="tpu_custom_call" | custom-call | tf_op jit(solution)/shard_map/exchange/pallas_call | solution.py:523
  187.6 2.3 %copy.7 = bf16[2,4096,64]{1,2,0:T(8,128)(2,1)} copy(bf16[2,4096,64]{1,2,0:T(8,128)(2,1)} %bitcast.5) | data formatting | bytes 2097152
Async XLA Ops:
  61.9 0.8 copy-start.5
  62.7 0.7 copy-start.7
  72.3 1.0 copy-start.2
  73.4 81.0 %copy-start.8 = (s32[24,128]{1,0:T(8,128)S(1)}, s32[24,128]{1,0:T(8,128)}, u32[]{:S(2)}) copy-start(s32[24,128]{1,0:T(8,128)} %places.1) | copy-start | bytes 36868
  127.7 0.8 copy-start.4
  128.5 0.7 copy-start.6
  136.5 2.8 %copy-start = (bf16[3072,1024]{1,0:T(8,128)(2,1)S(1)}, bf16[3072,1024]{1,0:T(8,128)(2,1)}, u32[]{:S(2)}) copy-start(bf16[3072,1024]{1,0:T(8,128)(2,1)} %slab.5) | copy-start | bytes 18874372
  139.3 1.0 copy-start.3
  162.3 1.0 copy-start.1

commit v2 on v1

v2 whole, which is shorter than its diff:
```python
import functools

import jax
import jax.numpy as jnp
from jax import lax
from jax.experimental import pallas as pl
from jax.experimental.pallas import tpu as pltpu
from jax.sharding import Mesh
from jax.sharding import PartitionSpec as P

ITERS = 2
CAP = 128
NC = 6
NP = 4
NS = 2
TOL = 2e-3
COARSE = 1.0
STEPS = 14
F32 = jnp.float32
BF16 = jnp.bfloat16
MESH = pl.DeviceIdType.MESH
VMEM = pl.BlockSpec(memory_space=pltpu.VMEM)
SMEM = pl.BlockSpec(memory_space=pltpu.SMEM)
FEAT = ("xl", "core")


def nn(a, b):
    return lax.dot_general(a, b, (((1,), (0,)), ((), ())), preferred_element_type=F32)


def nt(a, b):
    return lax.dot_general(a, b, (((1,), (1,)), ((), ())), preferred_element_type=F32)


def tn(a, b):
    return lax.dot_general(a, b, (((0,), (0,)), ((), ())), preferred_element_type=F32)


def greet(targets):
    barrier = pltpu.get_barrier_semaphore()
    for target in targets:
        pl.semaphore_signal(barrier, inc=1, device_id=target, device_id_type=MESH)
    return barrier


def grid_of(rows):
    return (4, 4, 2) if rows == 32 else (2, rows // 4, 2)


def shifted(me, rows, shift):
    nz, ny, nx = grid_of(rows)
    z, y, x = me // (ny * nx), (me // nx) % ny, me % nx
    dz, dy, dx = shift
    return ((z + dz) % nz) * (ny * nx) + ((y + dy) % ny) * nx + (x + dx) % nx


def axis_peers(me, rows):
    nz, ny, nx = grid_of(rows)
    shifts = [(d, 0, 0) for d in range(1, nz)] + [(0, d, 0) for d in range(1, ny)]
    shifts += [(0, 0, d) for d in range(1, nx)]
    return [{"rows": shifted(me, rows, shift)} for shift in shifts]


def each_peer(me, rows, body):
    nz, ny, nx = grid_of(rows)
    fz, fy, fx = nz // 2, ny // 2, nx // 2

    def step(i):
        dz = (fz + i // (ny * nx)) % nz
        dy = (fy + (i // nx) % ny) % ny
        dx = (fx + i % nx) % nx
        there = shifted(me, rows, (dz, dy, dx))
        back = shifted(me, rows, (nz - dz, ny - dy, nx - dx))
        body(i, there, back)

    own = ((nz - fz) % nz) * ny * nx + ((ny - fy) % ny) * nx + (nx - fx) % nx
    pl.loop(0, own)(step)
    if own + 1 < rows:
        pl.loop(own + 1, rows)(step)


def remote(src, dst, send, recv, target):
    return pltpu.make_async_remote_copy(
        src_ref=src, dst_ref=dst, send_sem=send, recv_sem=recv, device_id=target, device_id_type=MESH
    )


def find_places(clusters, ids, place):
    blocks = ids.shape[0]
    lane = lax.broadcasted_iota(jnp.int32, (CAP, CAP), 1)
    sub = lax.broadcasted_iota(jnp.int32, (CAP, CAP), 0)
    before = jnp.where(sub < lane, F32(1), F32(0)).astype(BF16)
    names = lax.broadcasted_iota(jnp.int32, (clusters, CAP), 0)
    seen = jnp.zeros((clusters, 1), F32)
    for b in range(blocks):
        block = ids[b:b + 1, :]
        hot = jnp.where(names == block, F32(1), F32(0))
        earlier = nn(hot.astype(BF16), before) + seen
        slot = jnp.sum(hot * earlier, axis=0, keepdims=True).astype(jnp.int32)
        pair = block // 2
        odd = block - 2 * pair
        place[b:b + 1, :] = odd * (clusters // 2 * CAP) + pair * CAP + slot
        seen = seen + jnp.sum(hot, axis=1, keepdims=True)


def covariance_kernel(rows, first, *refs):
    if first:
        slab, q, ids, z_out, gram_out, place, *refs = refs
    else:
        slab, q, z_out, gram_out, *refs = refs
    (qb, total, away, home, part, mine, theirs, y, z, z_send, z_recv, z_full, g_part, g_near, g_mine, g_far, g_all,
     near_sem, far_sem, y_sem, rs_sem, ag_sem, g_sem, round_a, round_b) = refs
    me, core, xl = lax.axis_index("rows"), lax.axis_index("core"), lax.axis_index("xl")
    near, far = {"core": 1 - core}, {"xl": 1 - xl}
    chunk = slab.shape[0] // (2 * NC)
    half_rows = NC * chunk
    width = q.shape[1]
    peers = axis_peers(me, rows)
    barrier = greet([near, far] + peers)
    qb[...] = q[...].astype(BF16)

    def held(h, i):
        return slab[pl.ds(pl.multiple_of(h * half_rows + i * chunk, chunk), chunk), :]

    def to_near(i):
        return remote(away.at[i], home.at[i], near_sem.at[0, i], near_sem.at[1, i], near)

    def to_far(i):
        return remote(mine.at[i], theirs.at[i], far_sem.at[0, i], far_sem.at[1, i], far)

    def share(i):
        return remote(y.at[core, i], y.at[core, i], y_sem.at[0, i], y_sem.at[1, i], near)

    def shared(i):
        return remote(y.at[1 - core, i], y.at[1 - core, i], y_sem.at[0, i], y_sem.at[1, i], near)

    def chip_sum(i):
        to_near(i).wait_recv()
        mine[i] = (part[i] + home[i].astype(F32)).astype(BF16)
        to_far(i).start()

    def pass_on(sem):
        for peer in peers:
            pl.semaphore_signal(sem, inc=1, device_id=peer, device_id_type=MESH)

    for i in range(NC):
        away[i] = nn(held(1 - core, i), qb[...]).astype(BF16)
        if i == 0:
            pl.semaphore_wait(barrier, len(peers) + 2)
        to_near(i).start()
        part[i] = nn(held(core, i), qb[...])
        if i > 0:
            chip_sum(i - 1)
        if i == 1:
            pass_on(round_a)
    chip_sum(NC - 1)
    pl.semaphore_wait(round_a, len(peers))
    pass_on(round_b)
    if first:
        find_places(2 * rows, ids, place)
    pl.semaphore_wait(round_b, len(peers))

    def add(h, i, start=False):
        term = tn(y[h, i], held(h, i))
        z[...] = term if start else z[...] + term

    for i in range(NC):
        to_far(i).wait_recv()
        y[core, i] = (mine[i].astype(F32) + theirs[i].astype(F32)).astype(BF16)
        share(i).start()
        add(core, i, i == 0)
        if i > 0:
            shared(i - 1).wait_recv()
            add(1 - core, i - 1)
    shared(NC - 1).wait_recv()
    add(1 - core, NC - 1)

    deep, wide = z_send.shape[2:]
    group = rows // 2
    for s in range(NS):
        for p in range(rows):
            f, k = divmod(p, group)
            left = (f * NS + s) * wide
            z_send[s, p] = z[k * deep:(k + 1) * deep, left:left + wide].astype(BF16)

    def scatter(s, slot, there):
        return remote(z_send.at[s, there], z_recv.at[s, slot], rs_sem.at[0, s, slot], rs_sem.at[1, s, slot],
                      {"rows": there})

    def gather(s, slot, owner, there):
        return remote(z_full.at[s, owner], z_full.at[s, owner], ag_sem.at[0, s, slot], ag_sem.at[1, s, slot],
                      {"rows": there})

    for s in range(NS):
        each_peer(me, rows, lambda i, there, back: scatter(s, i, there).start())
    for s in range(NS):
        total[...] = z_send[s, me].astype(F32)

        def more(i, there, back):
            scatter(s, i, there).wait_recv()
            total[...] = total[...] + z_recv[s, i].astype(F32)

        each_peer(me, rows, more)
        z_full[s, me] = total[...].astype(BF16)
        each_peer(me, rows, lambda i, there, back: gather(s, i, me, there).start())

    half = width // 2
    for s in range(NS):
        each_peer(me, rows, lambda i, there, back: gather(s, i, back, there).wait_recv())
        for f in range(2):
            block = z_full[s, f * group:(f + 1) * group].reshape(width, wide)
            term = nt(block, block).reshape(2, half, width)
            g_part[...] = term if s + f == 0 else g_part[...] + term
    out_near = remote(g_part.at[1 - core], g_near, g_sem.at[0, 0], g_sem.at[1, 0], near)
    out_far = remote(g_mine, g_far, g_sem.at[0, 1], g_sem.at[1, 1], far)
    out_back = remote(g_all.at[core], g_all.at[core], g_sem.at[0, 2], g_sem.at[1, 2], near)
    in_back = remote(g_all.at[1 - core], g_all.at[1 - core], g_sem.at[0, 2], g_sem.at[1, 2], near)
    out_near.start()
    z_out[...] = z_full[...]
    out_near.wait_recv()
    g_mine[...] = g_part[core] + g_near[...]
    out_far.start()
    out_far.wait_recv()
    g_all[core] = g_mine[...] + g_far[...]
    out_back.start()
    in_back.wait_recv()
    gram_out[...] = g_all[...].reshape(width, width)
    for i in range(NC):
        to_near(i).wait_send()
        to_far(i).wait_send()
        share(i).wait_send()
    for s in range(NS):
        def sent(i, there, back):
            scatter(s, i, there).wait_send()
            gather(s, i, me, there).wait_send()

        each_peer(me, rows, sent)
    out_near.wait_send()
    out_far.wait_send()
    out_back.wait_send()


def covariance(slab, q, rows, ident, ids=None):
    length, feats = slab.shape
    width = q.shape[1]
    chunk = length // (2 * NC)
    piece = (2 * width // rows, feats // (2 * NS))
    half = (width // 2, width)
    dma = pltpu.SemaphoreType.DMA
    first = ids is not None
    out = [jax.ShapeDtypeStruct((NS, rows, *piece), BF16), jax.ShapeDtypeStruct((width, width), F32)]
    args = [slab, q]
    if first:
        out.append(jax.ShapeDtypeStruct(ids.shape, jnp.int32))
        args.append(ids)
    return pl.pallas_call(
        functools.partial(covariance_kernel, rows, first),
        out_shape=out,
        in_specs=[VMEM] * len(args),
        out_specs=[VMEM] * len(out),
        scratch_shapes=[
            pltpu.VMEM(q.shape, BF16),
            pltpu.VMEM(piece, F32),
            pltpu.VMEM((NC, chunk, width), BF16),
            pltpu.VMEM((NC, chunk, width), BF16),
            pltpu.VMEM((NC, chunk, width), F32),
            pltpu.VMEM((NC, chunk, width), BF16),
            pltpu.VMEM((NC, chunk, width), BF16),
            pltpu.VMEM((2, NC, chunk, width), BF16),
            pltpu.VMEM((width, feats), F32),
            pltpu.VMEM((NS, rows, *piece), BF16),
            pltpu.VMEM((NS, rows, *piece), BF16),
            pltpu.VMEM((NS, rows, *piece), BF16),
            pltpu.VMEM((2, *half), F32),
            pltpu.VMEM(half, F32),
            pltpu.VMEM(half, F32),
            pltpu.VMEM(half, F32),
            pltpu.VMEM((2, *half), F32),
            dma((2, NC)),
            dma((2, NC)),
            dma((2, NC)),
            dma((2, NS, rows)),
            dma((2, NS, rows)),
            dma((2, 3)),
            pltpu.SemaphoreType.REGULAR,
            pltpu.SemaphoreType.REGULAR,
        ],
        compiler_params=pltpu.CompilerParams(
            collective_id=ident, has_side_effects=True, vmem_limit_bytes=32 << 20
        ),
        name="covariance",
    )(*args)


def split(a):
    top = a.astype(BF16)
    return top, (a - top.astype(F32)).astype(BF16)


def fine(dot, a, b):
    (a0, a1), (b0, b1) = split(a), split(b)
    return dot(a0, b0) + (dot(a0, b1) + dot(a1, b0))


def basis_kernel(last, kept, gram, z, q_out, unit, x, e, a, state):
    n = gram.shape[0]
    row = lax.broadcasted_iota(jnp.int32, (n, n), 0)
    col = lax.broadcasted_iota(jnp.int32, (n, n), 1)
    lower = jnp.where(row > col, F32(1), jnp.where(row == col, F32(0.5), F32(0)))
    eye = jnp.where(row == col, F32(1), F32(0))

    g = gram[...]
    diag = g * eye
    across = lax.rsqrt(jnp.sum(diag, axis=0, keepdims=True))
    down = lax.rsqrt(jnp.sum(diag, axis=1, keepdims=True))
    scaled = g * across * down
    unit[...] = scaled
    begin = scaled - eye
    e[...] = begin
    x[...] = eye
    state[0] = 0

    @pl.loop(0, STEPS)
    def _(step):
        @pl.when(state[0] == 0)
        def _():
            now = e[...]
            size = jnp.sum(now * now)
            better = x[...] - nn((now * lower).astype(BF16), x[...].astype(BF16))
            x[...] = better
            done = size < TOL * TOL
            state[0] = done.astype(jnp.int32)

            @pl.when(size > COARSE * COARSE)
            def _():
                near = better.astype(BF16)
                e[...] = nt(nn(near, unit[...].astype(BF16)).astype(BF16), near) - eye

            @pl.when(jnp.logical_not(done) & jnp.logical_not(size > COARSE * COARSE))
            def _():
                e[...] = fine(nt, fine(nn, better, unit[...]), better) - eye

    @pl.when(state[0] == 0)
    def _():
        a[...] = unit[...]
        x[...] = eye

        @pl.loop(0, n)
        def _(j):
            pick_row = row == j
            pick_col = col == j
            now = a[...]
            inv = x[...]
            a_row = jnp.sum(jnp.where(pick_row, now, 0.0), axis=0, keepdims=True)
            a_col = jnp.sum(jnp.where(pick_col, now, 0.0), axis=1, keepdims=True)
            x_row = jnp.sum(jnp.where(pick_row, inv, 0.0), axis=0, keepdims=True)
            pivot = jnp.sum(jnp.where(pick_row & pick_col, now, 0.0))
            root = jnp.sqrt(jnp.full((1, n), pivot))
            line = x_row / root
            factor = jnp.where(row[:, :1] > j, a_col / root[:, :1], 0.0)
            x[...] = jnp.where(pick_row, line, inv - factor * line)
            a[...] = now - factor * (a_row / root)

    top, rest = split(x[...] * across)
    ns, rows, _, wide = z.shape
    group = rows // 2
    for f in range(2):
        for s in range(ns):
            block = z[s, f * group:(f + 1) * group].reshape(n, wide)
            qt = nn(top, block) + nn(rest, block)
            if last:
                index = lax.broadcasted_iota(jnp.int32, (n, wide), 0)
                qt = jnp.where(index < kept[0], qt, 0.0)
            left = (f * ns + s) * wide
            q_out[left:left + wide, :] = qt.T.astype(BF16)


def new_basis(kept, gram, z, last):
    n = gram.shape[0]
    return pl.pallas_call(
        functools.partial(basis_kernel, last),
        out_shape=jax.ShapeDtypeStruct((2 * z.shape[0] * z.shape[3], n), BF16),
        in_specs=[SMEM, VMEM, VMEM],
        out_specs=VMEM,
        scratch_shapes=[pltpu.VMEM((n, n), F32)] * 4 + [pltpu.SMEM((2,), jnp.int32)],
        compiler_params=pltpu.CompilerParams(vmem_limit_bytes=24 << 20),
        name="new_basis",
    )(kept, gram, z)


def project_kernel(slab, q, p_out, away, home, part, keep, send, recv, p,
                   near_sem, far_sem, p_sem):
    core, xl = lax.axis_index("core"), lax.axis_index("xl")
    near, far = {"core": 1 - core}, {"xl": 1 - xl}
    chunk = slab.shape[0] // (2 * NP)
    width = q.shape[1]
    half = width // 2
    barrier = greet((near, far))

    def held(h, i):
        return slab[pl.ds(pl.multiple_of(h * NP * chunk + i * chunk, chunk), chunk), :]

    def to_near(i):
        return remote(away.at[i], home.at[i], near_sem.at[0, i], near_sem.at[1, i], near)

    def to_far(i):
        return remote(send.at[i], recv.at[i], far_sem.at[0, i], far_sem.at[1, i], far)

    def share(i):
        return remote(p.at[core, i], p.at[core, i], p_sem.at[0, i], p_sem.at[1, i], near)

    def shared(i):
        return remote(p.at[1 - core, i], p.at[1 - core, i], p_sem.at[0, i], p_sem.at[1, i], near)

    def chip_sum(i):
        to_near(i).wait_recv()
        both = part[i] + home[i].astype(F32)
        low, high = both[:, :half], both[:, half:]
        keep[i] = jnp.where(xl == 0, low, high)
        send[i] = jnp.where(xl == 0, high, low).astype(BF16)
        to_far(i).start()

    for i in range(NP):
        away[i] = nn(held(1 - core, i), q[...]).astype(BF16)
        if i == 0:
            pl.semaphore_wait(barrier, 2)
        to_near(i).start()
        part[i] = nn(held(core, i), q[...])
        if i > 0:
            chip_sum(i - 1)
    chip_sum(NP - 1)
    for i in range(NP):
        to_far(i).wait_recv()
        p[core, i] = (keep[i] + recv[i].astype(F32)).astype(BF16)
        share(i).start()
    for i in range(NP):
        shared(i).wait_recv()
    p_out[...] = p[...].reshape(p_out.shape)
    for i in range(NP):
        to_near(i).wait_send()
        to_far(i).wait_send()
        share(i).wait_send()


def project(slab, q, ident):
    length = slab.shape[0]
    width = q.shape[1]
    chunk = length // (2 * NP)
    half = width // 2
    dma = pltpu.SemaphoreType.DMA
    return pl.pallas_call(
        project_kernel,
        out_shape=jax.ShapeDtypeStruct((length, half), BF16),
        in_specs=[VMEM, VMEM],
        out_specs=VMEM,
        scratch_shapes=[
            pltpu.VMEM((NP, chunk, width), BF16),
            pltpu.VMEM((NP, chunk, width), BF16),
            pltpu.VMEM((NP, chunk, width), F32),
            pltpu.VMEM((NP, chunk, half), F32),
            pltpu.VMEM((NP, chunk, half), BF16),
            pltpu.VMEM((NP, chunk, half), BF16),
            pltpu.VMEM((2, NP, chunk, half), BF16),
            dma((2, NP)),
            dma((2, NP)),
            dma((2, NP)),
        ],
        compiler_params=pltpu.CompilerParams(
            collective_id=ident, has_side_effects=True, vmem_limit_bytes=24 << 20
        ),
        name="project",
    )(slab, q)


def pack_kernel(place, side, p, out, doubled, spread):
    rows = out.shape[0]
    length, lanes = p.shape
    cols = lanes // 2
    unroll = 16
    low = lax.broadcasted_iota(jnp.int32, (length, lanes), 1) < cols
    wide = p[...].astype(F32)
    turned = pltpu.roll(wide, cols, 1)
    doubled[...] = jnp.where(low == (side[0] == 0), wide, turned)
    spread[...] = jnp.zeros_like(spread)

    @pl.loop(0, length // unroll)
    def _(step):
        for u in range(unroll):
            i = step * unroll + u
            spread[pl.ds(place[i], 1), :] = doubled[pl.ds(i, 1), :]

    even = lax.broadcasted_iota(jnp.int32, (CAP, lanes), 1) < cols

    @pl.loop(0, rows)
    def _(r):
        start = pl.multiple_of(r * CAP, CAP)
        first = spread[pl.ds(start, CAP), :]
        second = spread[pl.ds(pl.multiple_of(rows * CAP + start, CAP), CAP), :]
        out[r] = jnp.where(even, first, second).T.astype(BF16)


def packed_rows(place, side, p, rows):
    length, lanes = p.shape
    return pl.pallas_call(
        pack_kernel,
        out_shape=jax.ShapeDtypeStruct((rows, lanes, CAP), BF16),
        in_specs=[SMEM, SMEM, VMEM],
        out_specs=VMEM,
        scratch_shapes=[pltpu.VMEM((length, lanes), F32), pltpu.VMEM((2 * rows * CAP, lanes), F32)],
        compiler_params=pltpu.CompilerParams(vmem_limit_bytes=32 << 20),
        name="packed_rows",
    )(place, side, p)


def exchange_kernel(rows, buf, out, arrived, sem):
    me = lax.axis_index("rows")
    barrier = pltpu.get_barrier_semaphore()

    def hello(i, there, back):
        pl.semaphore_signal(barrier, inc=1, device_id={"rows": there}, device_id_type=MESH)

    each_peer(me, rows, hello)
    pl.semaphore_wait(barrier, rows - 1)

    def send(i, there, at):
        return remote(buf.at[there], arrived.at[at], sem.at[0, i], sem.at[1, i], {"rows": there})

    each_peer(me, rows, lambda i, there, back: send(i, there, me).start())
    arrived[me] = buf[me]
    each_peer(me, rows, lambda i, there, back: send(i, there, back).wait_recv())
    out[...] = arrived[...]
    each_peer(me, rows, lambda i, there, back: send(i, there, me).wait_send())


def exchange(buf, ident):
    rows = buf.shape[0]
    return pl.pallas_call(
        functools.partial(exchange_kernel, rows),
        out_shape=jax.ShapeDtypeStruct(buf.shape, BF16),
        in_specs=[VMEM],
        out_specs=VMEM,
        scratch_shapes=[pltpu.VMEM(buf.shape, BF16), pltpu.SemaphoreType.DMA((2, rows))],
        compiler_params=pltpu.CompilerParams(
            collective_id=ident, has_side_effects=True, vmem_limit_bytes=16 << 20
        ),
        name="exchange",
    )(buf)


def arrange_kernel(arrived, out):
    cols = out.shape[1]
    for r in range(arrived.shape[0]):
        for h in range(2):
            out[h, :, r * CAP:(r + 1) * CAP] = arrived[r, h * cols:(h + 1) * cols, :]


def arrange(arrived):
    rows, lanes, _ = arrived.shape
    return pl.pallas_call(
        arrange_kernel,
        out_shape=jax.ShapeDtypeStruct((2, lanes // 2, rows * CAP), BF16),
        in_specs=[VMEM],
        out_specs=VMEM,
        compiler_params=pltpu.CompilerParams(vmem_limit_bytes=16 << 20),
        name="arrange",
    )(arrived)


def shards(rows, slab, basis, cluster_ids, kept):
    side = jnp.broadcast_to(lax.axis_index("core"), (1,)).astype(jnp.int32)
    z, gram, place = covariance(slab, basis, rows, 0, cluster_ids.reshape(-1, CAP))
    for step in range(1, ITERS):
        q = new_basis(kept, gram, z, False)
        z, gram = covariance(slab, q, rows, step)
    q = new_basis(kept, gram, z, True)
    p = project(slab, q, ITERS)
    buf = packed_rows(place.reshape(-1), side, p, rows)
    return jnp.swapaxes(arrange(exchange(buf, ITERS + 1)), 1, 2)


def solution(mesh):
    rows = mesh.shape["rows"]
    torus = Mesh(mesh.devices.reshape(rows, 2, 2), ("rows", "xl", "core"))
    placed = (P("rows", FEAT), P(FEAT, None), P("rows", None), P())
    return jax.shard_map(
        functools.partial(shards, rows), mesh=torus, in_specs=placed,
        out_specs=P("rows", None, FEAT), check_vma=False,
    )
```

time: 191 us -> 166 us (0.87)
  Pallas kernels: 177 us -> 160 us
  local copies, waits for them, and re-layouts: 11.1 us -> 4.71 us
    pallas_call x2, Pallas kernels: 16.2 us -> 7.29 us  [new_basis(): pl.pallas_call(functools.partial(basis_kernel, last), out_shape=jax.Shape...]
    pallas_call x3, Pallas kernels: 114 us -> 108 us  [the longest x2 106 us: covariance(): pl.pallas_call(functools.partial(covariance_kernel, rows, first), out_sha...]
    unnamed x19 -> x6, local copies, waits for them, and re-layouts: 11.1 us -> 4.71 us
where the time goes in v2:
time: 166 us
  Pallas kernels  160 us (96%)
  local copies, waits for them, and re-layouts  4.71 us (3%)
    pallas_call x2, Pallas kernels, covariance(): pl.pallas_call(functools.partial(covariance_kernel, rows, first), out_sha...  106 us
    pallas_call x1, Pallas kernels, exchange(): pl.pallas_call(functools.partial(exchange_kernel, rows), out_shape=jax.Sh...  23.3 us
    pallas_call x1, Pallas kernels, project(): pl.pallas_call(project_kernel, out_shape=jax.ShapeDtypeStruct((length, ha...  14.2 us
    pallas_call x1, Pallas kernels, packed_rows(): pl.pallas_call(pack_kernel, out_shape=jax.ShapeDtypeStruct((rows, lanes,...  7.89 us
    pallas_call x2, Pallas kernels, new_basis(): pl.pallas_call(functools.partial(basis_kernel, last), out_shape=jax.Shape...  7.29 us
    unnamed x6, local copies, waits for them, and re-layouts  4.71 us

profile of v2, /device:TPU:0, one launch (start us, length us, event | category | flops | bytes accessed | tf_op | source)
XLA Modules:
  0.0 165.8 jit_solution(9942242546332241975)
XLA Ops:
  0.7 0.0 copy-start
  0.7 2.8 %copy-done = bf16[3072,1024]{1,0:T(8,128)(2,1)S(1)} copy-done((bf16[3072,1024]{1,0:T(8,128)(2,1)S(1)}, bf16[3072,1024]{1,0:T(8,128)(2,1)}, u32[]{:S(2)}) %copy-start) | copy-done | bytes 6291480
  3.4 0.0 copy-start.1
  3.4 1.2 copy-done.1
  4.7 0.0 copy-start.2
  4.7 0.7 copy-done.2
  5.4 56.2 %covariance.2 = (bf16[2,32,16,256]{3,2,1,0:T(8,128)(2,1)S(1)}, f32[256,256]{1,0:T(8,128)S(1)}, s32[24,128]{1,0:T(8,128)S(1)}) custom-call(bf16[3072,1024]{1,0:T(8,128)(2,1)S(1)} %copy-done, f32[1024,256]{1,0:T(8,128)S(1)} %copy-done.1, s32[24,128]{1,0:T(8,128)S(1)} %bitcast.5), custom_call_target="tpu_custom_call" | custom-call | tf_op jit(solution)/shard_map/covariance/pallas_call | solution.py:256
  61.5 4.0 %new_basis.2.refs_1_ = bf16[1024,256]{1,0:T(8,128)(2,1)S(1)} custom-call(s32[1]{0:T(128)S(6)} %copy.5.kept, f32[256,256]{1,0:T(8,128)S(1)} %get-tuple-element.11.gram, bf16[2,32,16,256]{3,2,1,0:T(8,128)(2,1)S(1)} %get-tuple-element.12.z), custom_call_target="tpu_custom_call" | custom-call | tf_op jit(solution)/shard_map/new_basis/pallas_call | solution.py:380
  65.6 50.3 %covariance.3 = (bf16[2,32,16,256]{3,2,1,0:T(8,128)(2,1)S(1)}, f32[256,256]{1,0:T(8,128)S(1)}) custom-call(bf16[3072,1024]{1,0:T(8,128)(2,1)S(1)} %copy-done, bf16[1024,256]{1,0:T(8,128)(2,1)S(1)} %new_basis.2.refs_1_), custom_call_target="tpu_custom_call" | custom-call | tf_op jit(solution)/shard_map/covariance/pallas_call | solution.py:256
  115.9 3.3 %new_basis.3.q = bf16[1024,256]{1,0:T(8,128)(2,1)S(1)} custom-call(s32[1]{0:T(128)S(6)} %copy.5.kept, f32[256,256]{1,0:T(8,128)S(1)} %get-tuple-element.13.gram, bf16[2,32,16,256]{3,2,1,0:T(8,128)(2,1)S(1)} %get-tuple-element.14.z), custom_call_target="tpu_custom_call" | custom-call | tf_op jit(solution)/shard_map/new_basis/pallas_call | solution.py:380
  119.1 14.2 %project.1.p = bf16[3072,128]{1,0:T(8,128)(2,1)S(1)} custom-call(bf16[3072,1024]{1,0:T(8,128)(2,1)S(1)} %copy-done, bf16[1024,256]{1,0:T(8,128)(2,1)S(1)} %new_basis.3.q), custom_call_target="tpu_custom_call" | custom-call | tf_op jit(solution)/shard_map/project/pallas_call | solution.py:451
  133.3 7.9 %packed_rows.1.buf = bf16[32,128,128]{2,1,0:T(8,128)(2,1)S(1)} custom-call(s32[3072]{0:T(1024)S(1)} %bitcast.4, s32[1]{0:T(128)} %bitcast.2.side, bf16[3072,128]{1,0:T(8,128)(2,1)S(1)} %project.1.p), custom_call_target="tpu_custom_call" | custom-call | tf_op jit(solution)/shard_map/packed_rows/pallas_call | solution.py:504
  141.2 23.3 %exchange.1.arrived = bf16[32,128,128]{2,1,0:T(8,128)(2,1)S(1)} custom-call(bf16[32,128,128]{2,1,0:T(8,128)(2,1)S(1)} %packed_rows.1.buf), custom_call_target="tpu_custom_call" | custom-call | tf_op jit(solution)/shard_map/exchange/pallas_call | solution.py:537
  164.6 1.2 arrange.1
Async XLA Ops:
  0.7 2.8 %copy-start = (bf16[3072,1024]{1,0:T(8,128)(2,1)S(1)}, bf16[3072,1024]{1,0:T(8,128)(2,1)}, u32[]{:S(2)}) copy-start(bf16[3072,1024]{1,0:T(8,128)(2,1)} %slab.1) | copy-start | bytes 18874372
  3.4 1.2 copy-start.1
  4.7 0.7 copy-start.2

commit v3 on v2

v3 whole, which is shorter than its diff:
```python
import functools

import jax
import jax.numpy as jnp
from jax import lax
from jax.experimental import pallas as pl
from jax.experimental.pallas import tpu as pltpu
from jax.sharding import Mesh
from jax.sharding import PartitionSpec as P

ITERS = 2
CAP = 128
SHARES = (1, 2, 2, 2, 2, 2, 1)
NP = 4
NS = 2
TOL = 2e-3
COARSE = 1.0
STEPS = 14
F32 = jnp.float32
BF16 = jnp.bfloat16
MESH = pl.DeviceIdType.MESH
VMEM = pl.BlockSpec(memory_space=pltpu.VMEM)
SMEM = pl.BlockSpec(memory_space=pltpu.SMEM)
HBM = pl.BlockSpec(memory_space=pltpu.HBM)
FEAT = ("xl", "core")


def nn(a, b):
    return lax.dot_general(a, b, (((1,), (0,)), ((), ())), preferred_element_type=F32)


def nt(a, b):
    return lax.dot_general(a, b, (((1,), (1,)), ((), ())), preferred_element_type=F32)


def tn(a, b):
    return lax.dot_general(a, b, (((0,), (0,)), ((), ())), preferred_element_type=F32)


def greet(targets):
    barrier = pltpu.get_barrier_semaphore()
    for target in targets:
        pl.semaphore_signal(barrier, inc=1, device_id=target, device_id_type=MESH)
    return barrier


def grid_of(rows):
    return (4, 4, 2) if rows == 32 else (2, rows // 4, 2)


def terms(me, rows):
    nz, ny, nx = grid_of(rows)
    z, y, x = me // (ny * nx), (me // nx) % ny, me % nx
    along_z = [((z + d) % nz) * (ny * nx) for d in range(nz)]
    along_y = [((y + d) % ny) * nx for d in range(ny)]
    return along_z, along_y, [(x + d) % nx for d in range(nx)]


def axis_peers(me, rows):
    az, ay, ax = terms(me, rows)
    return ([{"rows": a + ay[0] + ax[0]} for a in az[1:]] + [{"rows": az[0] + a + ax[0]} for a in ay[1:]]
            + [{"rows": az[0] + ay[0] + a} for a in ax[1:]])


def peers_of(me, rows):
    lists = terms(me, rows)

    def order(n):
        return sorted(range(n), key=lambda d: -min(d, n - d))

    found = []
    for dz in order(len(lists[0])):
        for dy in order(len(lists[1])):
            for dx in order(len(lists[2])):
                if dz or dy or dx:
                    there = lists[0][dz] + lists[1][dy] + lists[2][dx]
                    back = lists[0][-dz] + lists[1][-dy] + lists[2][-dx]
                    found.append((len(found), there, back))
    return found


def chunks_of(half):
    unit = half // sum(SHARES)
    found, start = [], 0
    for share in SHARES:
        found.append((start, share * unit))
        start += share * unit
    return found


def remote(src, dst, send, recv, target):
    return pltpu.make_async_remote_copy(
        src_ref=src, dst_ref=dst, send_sem=send, recv_sem=recv, device_id=target, device_id_type=MESH
    )


def find_places(clusters, ids, place):
    blocks = ids.shape[0]
    lane = lax.broadcasted_iota(jnp.int32, (CAP, CAP), 1)
    sub = lax.broadcasted_iota(jnp.int32, (CAP, CAP), 0)
    before = jnp.where(sub < lane, F32(1), F32(0)).astype(BF16)
    names = lax.broadcasted_iota(jnp.int32, (clusters, CAP), 0)
    seen = jnp.zeros((clusters, 1), F32)
    for b in range(blocks):
        block = ids[b:b + 1, :]
        hot = jnp.where(names == block, F32(1), F32(0))
        earlier = nn(hot.astype(BF16), before) + seen
        slot = jnp.sum(hot * earlier, axis=0, keepdims=True).astype(jnp.int32)
        pair = block // 2
        odd = block - 2 * pair
        place[b:b + 1, :] = odd * (clusters // 2 * CAP) + pair * CAP + slot
        seen = seen + jnp.sum(hot, axis=1, keepdims=True)


def covariance_kernel(rows, first, *refs):
    if first:
        source, basis, names, z_out, gram_out, place, q, ids, *refs = refs
    else:
        source, q, z_out, gram_out, *refs = refs
    (slab, load_sem, qb, away, home, part, mine, theirs, y, z, z_send, z_recv, z_full, g_part, g_near, g_mine, g_far, g_all,
     near_sem, far_sem, y_sem, rs_sem, ag_sem, g_sem, round_a, round_b) = refs
    me, core, xl = lax.axis_index("rows"), lax.axis_index("core"), lax.axis_index("xl")
    near, far = {"core": 1 - core}, {"xl": 1 - xl}
    half_rows = slab.shape[0] // 2
    width = q.shape[1]
    chunks = chunks_of(half_rows)
    count = len(chunks)
    beside = axis_peers(me, rows)
    barrier = greet([near, far] + beside)

    def rows_at(h, i):
        start, size = chunks[i]
        return pl.ds(pl.multiple_of(h * half_rows + start, 8), size)

    def load(own, i):
        at = rows_at(core if own else 1 - core, i)
        return pltpu.make_async_copy(source.at[at], slab.at[at], load_sem.at[own, i])

    for i in range(count):
        load(0, i).start()
        load(1, i).start()
    if first:
        begin = pltpu.make_async_copy(basis, q, load_sem.at[0, count])
        naming = pltpu.make_async_copy(names, ids, load_sem.at[1, count])
        begin.start()
        naming.start()
        begin.wait()

    def held(own, i):
        return slab[rows_at(core if own else 1 - core, i), :]

    def scores(own, i):
        load(own, i).wait()
        return nn(held(own, i), qb[...])

    def at(ref, i):
        start, size = chunks[i]
        return ref.at[pl.ds(start, size)]

    def to_near(i):
        return remote(at(away, i), at(home, i), near_sem.at[0, i], near_sem.at[1, i], near)

    def to_far(i):
        return remote(at(mine, i), at(theirs, i), far_sem.at[0, i], far_sem.at[1, i], far)

    def y_at(own, i):
        return at(y.at[core if own else 1 - core], i)

    def share(i):
        return remote(y_at(1, i), y_at(1, i), y_sem.at[0, i], y_sem.at[1, i], near)

    def shared(i):
        return remote(y_at(0, i), y_at(0, i), y_sem.at[0, i], y_sem.at[1, i], near)

    def chip_sum(i):
        to_near(i).wait_recv()
        at(mine, i)[...] = (at(part, i)[...] + at(home, i)[...].astype(F32)).astype(BF16)
        to_far(i).start()

    def pass_on(sem):
        for peer in beside:
            pl.semaphore_signal(sem, inc=1, device_id=peer, device_id_type=MESH)

    qb[...] = q[...].astype(BF16)
    for i in range(count):
        at(away, i)[...] = scores(0, i).astype(BF16)
        if i == 0:
            at(part, i)[...] = scores(1, i)
            continue
        if i == 1:
            pl.semaphore_wait(barrier, len(beside) + 2)
            to_near(0).start()
        to_near(i).start()
        at(part, i)[...] = scores(1, i)
        chip_sum(i - 1)
        if i == 2:
            pass_on(round_a)
    chip_sum(count - 1)
    pl.semaphore_wait(round_a, len(beside))
    pass_on(round_b)
    if first:
        naming.wait()
        find_places(2 * rows, ids, place)
    pl.semaphore_wait(round_b, len(beside))

    def add(own, i, start=False):
        term = tn(y_at(own, i)[...], held(own, i))
        z[...] = term if start else z[...] + term

    for i in range(count):
        to_far(i).wait_recv()
        y_at(1, i)[...] = (at(mine, i)[...].astype(F32) + at(theirs, i)[...].astype(F32)).astype(BF16)
        share(i).start()
        add(1, i, i == 0)
        if i > 0:
            shared(i - 1).wait_recv()
            add(0, i - 1)
    shared(count - 1).wait_recv()
    add(0, count - 1)

    deep, wide = z_send.shape[2:]
    group = rows // 2
    peers = peers_of(me, rows)

    def scatter(s, slot, there):
        return remote(z_send.at[s, there], z_recv.at[s, slot], rs_sem.at[0, s, slot], rs_sem.at[1, s, slot],
                      {"rows": there})

    def gather(s, slot, owner, there):
        return remote(z_full.at[s, owner], z_full.at[s, owner], ag_sem.at[0, s, slot], ag_sem.at[1, s, slot],
                      {"rows": there})

    for s in range(NS):
        for p in range(rows):
            f, k = divmod(p, group)
            left = (f * NS + s) * wide
            z_send[s, p] = z[k * deep:(k + 1) * deep, left:left + wide].astype(BF16)
        for slot, there, _ in peers:
            scatter(s, slot, there).start()
    for s in range(NS):
        total = z_send[s, me].astype(F32)
        for slot, there, _ in reversed(peers):
            scatter(s, slot, there).wait_recv()
            total = total + z_recv[s, slot].astype(F32)
        z_full[s, me] = total.astype(BF16)
        for slot, there, _ in peers:
            gather(s, slot, me, there).start()

    low = width // 2
    part_rows = low // 2
    for s in range(NS):
        for slot, there, back in reversed(peers):
            gather(s, slot, back, there).wait_recv()
        for f in range(2):
            block = z_full[s, f * group:(f + 1) * group].reshape(width, wide)
            terms_of = (nt(block[:low], block[:low]), nt(block[low:], block[:low]), nt(block[low:], block[low:]))
            for b, term in enumerate(terms_of):
                for h in range(2):
                    line = term[h * part_rows:(h + 1) * part_rows]
                    g_part[h, b] = line if s + f == 0 else g_part[h, b] + line
    out_near = remote(g_part.at[1 - core], g_near, g_sem.at[0, 0], g_sem.at[1, 0], near)
    out_far = remote(g_mine, g_far, g_sem.at[0, 1], g_sem.at[1, 1], far)
    out_back = remote(g_all.at[core], g_all.at[core], g_sem.at[0, 2], g_sem.at[1, 2], near)
    in_back = remote(g_all.at[1 - core], g_all.at[1 - core], g_sem.at[0, 2], g_sem.at[1, 2], near)
    out_near.start()
    z_out[...] = z_full[...]
    out_near.wait_recv()
    g_mine[...] = g_part[core] + g_near[...]
    out_far.start()
    for i in range(count):
        to_near(i).wait_send()
        to_far(i).wait_send()
        share(i).wait_send()
    for s in range(NS):
        for slot, there, _ in peers:
            scatter(s, slot, there).wait_send()
            gather(s, slot, me, there).wait_send()
    out_far.wait_recv()
    g_all[core] = g_mine[...] + g_far[...]
    out_back.start()
    in_back.wait_recv()
    for h in range(2):
        for b in range(3):
            gram_out[b, h * part_rows:(h + 1) * part_rows, :] = g_all[h, b]
    out_near.wait_send()
    out_far.wait_send()
    out_back.wait_send()


def covariance(slab, q, rows, ident, ids=None):
    length, feats = slab.shape
    width = q.shape[1]
    half = length // 2
    count = len(SHARES)
    piece = (2 * width // rows, feats // (2 * NS))
    low = width // 2
    parts = (3, low // 2, low)
    dma = pltpu.SemaphoreType.DMA
    first = ids is not None
    out = [jax.ShapeDtypeStruct((NS, rows, *piece), BF16), jax.ShapeDtypeStruct((3, low, low), F32)]
    args, extra, specs = [slab, q], [], [HBM, VMEM]
    if first:
        out.append(jax.ShapeDtypeStruct(ids.shape, jnp.int32))
        args.append(ids)
        extra = [pltpu.VMEM(q.shape, F32), pltpu.VMEM(ids.shape, jnp.int32)]
        specs = [HBM] * 3
    return pl.pallas_call(
        functools.partial(covariance_kernel, rows, first),
        out_shape=out,
        in_specs=specs,
        out_specs=[VMEM] * len(out),
        scratch_shapes=extra + [
            pltpu.VMEM(slab.shape, BF16),
            dma((2, count + 1)),
            pltpu.VMEM(q.shape, BF16),
            pltpu.VMEM((half, width), BF16),
            pltpu.VMEM((half, width), BF16),
            pltpu.VMEM((half, width), F32),
            pltpu.VMEM((half, width), BF16),
            pltpu.VMEM((half, width), BF16),
            pltpu.VMEM((2, half, width), BF16),
            pltpu.VMEM((width, feats), F32),
            pltpu.VMEM((NS, rows, *piece), BF16),
            pltpu.VMEM((NS, rows, *piece), BF16),
            pltpu.VMEM((NS, rows, *piece), BF16),
            pltpu.VMEM((2, *parts), F32),
            pltpu.VMEM(parts, F32),
            pltpu.VMEM(parts, F32),
            pltpu.VMEM(parts, F32),
            pltpu.VMEM((2, *parts), F32),
            dma((2, count)),
            dma((2, count)),
            dma((2, count)),
            dma((2, NS, rows)),
            dma((2, NS, rows)),
            dma((2, 3)),
            pltpu.SemaphoreType.REGULAR,
            pltpu.SemaphoreType.REGULAR,
        ],
        compiler_params=pltpu.CompilerParams(
            collective_id=ident, has_side_effects=True, vmem_limit_bytes=(53 if first else 52) << 20
        ),
        name="covariance",
    )(*args)


def split(a):
    top = a.astype(BF16)
    return top, (a - top.astype(F32)).astype(BF16)


def fine(dot, a, b):
    (a0, a1), (b0, b1) = split(a), split(b)
    return dot(a0, b0) + (dot(a0, b1) + dot(a1, b0))


def basis_kernel(last, kept, gram, z, q_out, unit, x, e, a, state):
    low = gram.shape[1]
    n = 2 * low
    row = lax.broadcasted_iota(jnp.int32, (n, n), 0)
    col = lax.broadcasted_iota(jnp.int32, (n, n), 1)
    lower = jnp.where(row > col, F32(1), jnp.where(row == col, F32(0.5), F32(0)))
    eye = jnp.where(row == col, F32(1), F32(0))

    x[:low, :low] = gram[0]
    x[low:, :low] = gram[1]
    x[low:, low:] = gram[2]
    x[:low, low:] = gram[1].T
    g = x[...]
    diag = g * eye
    across = lax.rsqrt(jnp.sum(diag, axis=0, keepdims=True))
    down = lax.rsqrt(jnp.sum(diag, axis=1, keepdims=True))
    scaled = g * across * down
    unit[...] = scaled
    begin = scaled - eye
    e[...] = begin
    x[...] = eye
    state[0] = 0

    @pl.loop(0, STEPS)
    def _(step):
        @pl.when(state[0] == 0)
        def _():
            now = e[...]
            size = jnp.sum(now * now)
            better = x[...] - nn((now * lower).astype(BF16), x[...].astype(BF16))
            x[...] = better
            done = size < TOL * TOL
            state[0] = done.astype(jnp.int32)

            @pl.when(size > COARSE * COARSE)
            def _():
                near = better.astype(BF16)
                e[...] = nt(nn(near, unit[...].astype(BF16)).astype(BF16), near) - eye

            @pl.when(jnp.logical_not(done) & jnp.logical_not(size > COARSE * COARSE))
            def _():
                e[...] = fine(nt, fine(nn, better, unit[...]), better) - eye

    @pl.when(state[0] == 0)
    def _():
        a[...] = unit[...]
        x[...] = eye

        @pl.loop(0, n)
        def _(j):
            pick_row = row == j
            pick_col = col == j
            now = a[...]
            inv = x[...]
            a_row = jnp.sum(jnp.where(pick_row, now, 0.0), axis=0, keepdims=True)
            a_col = jnp.sum(jnp.where(pick_col, now, 0.0), axis=1, keepdims=True)
            x_row = jnp.sum(jnp.where(pick_row, inv, 0.0), axis=0, keepdims=True)
            pivot = jnp.sum(jnp.where(pick_row & pick_col, now, 0.0))
            root = jnp.sqrt(jnp.full((1, n), pivot))
            line = x_row / root
            factor = jnp.where(row[:, :1] > j, a_col / root[:, :1], 0.0)
            x[...] = jnp.where(pick_row, line, inv - factor * line)
            a[...] = now - factor * (a_row / root)

    top, rest = split(x[...] * across)
    ns, rows, _, wide = z.shape
    group = rows // 2
    for f in range(2):
        for s in range(ns):
            block = z[s, f * group:(f + 1) * group].reshape(n, wide)
            qt = nn(top, block) + nn(rest, block)
            if last:
                index = lax.broadcasted_iota(jnp.int32, (n, wide), 0)
                qt = jnp.where(index < kept[0], qt, 0.0)
            left = (f * ns + s) * wide
            q_out[left:left + wide, :] = qt.T.astype(BF16)


def new_basis(kept, gram, z, last):
    n = 2 * gram.shape[1]
    return pl.pallas_call(
        functools.partial(basis_kernel, last),
        out_shape=jax.ShapeDtypeStruct((2 * z.shape[0] * z.shape[3], n), BF16),
        in_specs=[SMEM, VMEM, VMEM],
        out_specs=VMEM,
        scratch_shapes=[pltpu.VMEM((n, n), F32)] * 4 + [pltpu.SMEM((2,), jnp.int32)],
        compiler_params=pltpu.CompilerParams(vmem_limit_bytes=24 << 20),
        name="new_basis",
    )(kept, gram, z)


def project_kernel(source, q, p_out, slab, away, home, part, keep, send, recv, p,
                   load_sem, near_sem, far_sem, p_sem):
    core, xl = lax.axis_index("core"), lax.axis_index("xl")
    near, far = {"core": 1 - core}, {"xl": 1 - xl}
    chunk = source.shape[0] // (2 * NP)
    width = q.shape[1]
    half = width // 2
    barrier = greet((near, far))

    def load(own, i):
        h = core if own else 1 - core
        at = pl.ds(pl.multiple_of(h * NP * chunk + i * chunk, chunk), chunk)
        return pltpu.make_async_copy(source.at[at], slab.at[at], load_sem.at[own, i])

    for i in range(NP):
        load(0, i).start()
        load(1, i).start()

    def scores(own, i):
        load(own, i).wait()
        h = core if own else 1 - core
        return nn(slab[pl.ds(pl.multiple_of(h * NP * chunk + i * chunk, chunk), chunk), :], q[...])

    def to_near(i):
        return remote(away.at[i], home.at[i], near_sem.at[0, i], near_sem.at[1, i], near)

    def to_far(i):
        return remote(send.at[i], recv.at[i], far_sem.at[0, i], far_sem.at[1, i], far)

    def share(i):
        return remote(p.at[core, i], p.at[core, i], p_sem.at[0, i], p_sem.at[1, i], near)

    def shared(i):
        return remote(p.at[1 - core, i], p.at[1 - core, i], p_sem.at[0, i], p_sem.at[1, i], near)

    def chip_sum(i):
        to_near(i).wait_recv()
        both = part[i] + home[i].astype(F32)
        low, high = both[:, :half], both[:, half:]
        keep[i] = jnp.where(xl == 0, low, high)
        send[i] = jnp.where(xl == 0, high, low).astype(BF16)
        to_far(i).start()

    for i in range(NP):
        away[i] = scores(0, i).astype(BF16)
        if i == 0:
            pl.semaphore_wait(barrier, 2)
        to_near(i).start()
        part[i] = scores(1, i)
        if i > 0:
            chip_sum(i - 1)
    chip_sum(NP - 1)
    for i in range(NP):
        to_far(i).wait_recv()
        p[core, i] = (keep[i] + recv[i].astype(F32)).astype(BF16)
        share(i).start()
    for i in range(NP):
        shared(i).wait_recv()
    p_out[...] = p[...].reshape(p_out.shape)
    for i in range(NP):
        to_near(i).wait_send()
        to_far(i).wait_send()
        share(i).wait_send()


def project(slab, q, ident):
    length = slab.shape[0]
    width = q.shape[1]
    chunk = length // (2 * NP)
    half = width // 2
    dma = pltpu.SemaphoreType.DMA
    return pl.pallas_call(
        project_kernel,
        out_shape=jax.ShapeDtypeStruct((length, half), BF16),
        in_specs=[HBM, VMEM],
        out_specs=VMEM,
        scratch_shapes=[
            pltpu.VMEM(slab.shape, BF16),
            pltpu.VMEM((NP, chunk, width), BF16),
            pltpu.VMEM((NP, chunk, width), BF16),
            pltpu.VMEM((NP, chunk, width), F32),
            pltpu.VMEM((NP, chunk, half), F32),
            pltpu.VMEM((NP, chunk, half), BF16),
            pltpu.VMEM((NP, chunk, half), BF16),
            pltpu.VMEM((2, NP, chunk, half), BF16),
            dma((2, NP)),
            dma((2, NP)),
            dma((2, NP)),
            dma((2, NP)),
        ],
        compiler_params=pltpu.CompilerParams(
            collective_id=ident, has_side_effects=True, vmem_limit_bytes=52 << 20
        ),
        name="project",
    )(slab, q)


def pack_kernel(place, side, p, spread, doubled):
    length, lanes = p.shape
    cols = lanes // 2
    unroll = 16
    low = lax.broadcasted_iota(jnp.int32, (length, lanes), 1) < cols
    wide = p[...].astype(F32)
    turned = pltpu.roll(wide, cols, 1)
    doubled[...] = jnp.where(low == (side[0] == 0), wide, turned)
    spread[...] = jnp.zeros_like(spread)

    @pl.loop(0, length // unroll)
    def _(step):
        for u in range(unroll):
            i = step * unroll + u
            spread[pl.ds(place[i], 1), :] = doubled[pl.ds(i, 1), :]


def spread_rows(place, side, p, rows):
    length, lanes = p.shape
    return pl.pallas_call(
        pack_kernel,
        out_shape=jax.ShapeDtypeStruct((2 * rows * CAP, lanes), F32),
        in_specs=[SMEM, SMEM, VMEM],
        out_specs=VMEM,
        scratch_shapes=[pltpu.VMEM((length, lanes), F32)],
        compiler_params=pltpu.CompilerParams(vmem_limit_bytes=16 << 20),
        name="spread_rows",
    )(place, side, p)


def exchange_kernel(rows, spread, out, buf, arrived, sem):
    me = lax.axis_index("rows")
    lanes = spread.shape[1]
    peers = peers_of(me, rows)
    barrier = greet([{"rows": there} for _, there, _ in peers])
    even = lax.broadcasted_iota(jnp.int32, (CAP, lanes), 1) < lanes // 2

    def block(r):
        start = pl.multiple_of(r * CAP, CAP)
        low = spread[pl.ds(start, CAP), :]
        high = spread[pl.ds(pl.multiple_of(start + rows * CAP, CAP), CAP), :]
        return jnp.where(even, low, high).T.astype(BF16)

    def send(slot, there, at):
        return remote(buf.at[slot], arrived.at[at], sem.at[0, slot], sem.at[1, slot], {"rows": there})

    ahead = min(12, rows - 1)
    for slot, there, _ in peers[:ahead]:
        buf[slot] = block(there)
    pl.semaphore_wait(barrier, rows - 1)
    for slot, there, _ in peers:
        if slot >= ahead:
            buf[slot] = block(there)
        send(slot, there, me).start()
    out[me] = block(me)
    for slot, there, back in reversed(peers):
        send(slot, there, back).wait_recv()
        out[back] = arrived[back]
    for slot, there, _ in peers:
        send(slot, there, me).wait_send()


def exchange(spread, rows, ident):
    lanes = spread.shape[1]
    whole = (rows, lanes, CAP)
    return pl.pallas_call(
        functools.partial(exchange_kernel, rows),
        out_shape=jax.ShapeDtypeStruct(whole, BF16),
        in_specs=[VMEM],
        out_specs=VMEM,
        scratch_shapes=[
            pltpu.VMEM((rows - 1, lanes, CAP), BF16),
            pltpu.VMEM(whole, BF16),
            pltpu.SemaphoreType.DMA((2, rows - 1)),
        ],
        compiler_params=pltpu.CompilerParams(
            collective_id=ident, has_side_effects=True, vmem_limit_bytes=16 << 20
        ),
        name="exchange",
    )(spread)


def arrange_kernel(arrived, out):
    cols = out.shape[1]
    for r in range(arrived.shape[0]):
        for h in range(2):
            out[h, :, r * CAP:(r + 1) * CAP] = arrived[r, h * cols:(h + 1) * cols, :]


def arrange(arrived):
    rows, lanes, _ = arrived.shape
    return pl.pallas_call(
        arrange_kernel,
        out_shape=jax.ShapeDtypeStruct((2, lanes // 2, rows * CAP), BF16),
        in_specs=[VMEM],
        out_specs=VMEM,
        compiler_params=pltpu.CompilerParams(vmem_limit_bytes=16 << 20),
        name="arrange",
    )(arrived)


def shards(rows, slab, basis, cluster_ids, kept):
    side = jnp.broadcast_to(lax.axis_index("core"), (1,)).astype(jnp.int32)
    z, gram, place = covariance(slab, basis, rows, 0, cluster_ids.reshape(-1, CAP))
    for step in range(1, ITERS):
        q = new_basis(kept, gram, z, False)
        z, gram = covariance(slab, q, rows, step)
    q = new_basis(kept, gram, z, True)
    p = project(slab, q, ITERS)
    spread = spread_rows(place.reshape(-1), side, p, rows)
    return jnp.swapaxes(arrange(exchange(spread, rows, ITERS + 1)), 1, 2)


def solution(mesh):
    rows = mesh.shape["rows"]
    torus = Mesh(mesh.devices.reshape(rows, 2, 2), ("rows", "xl", "core"))
    placed = (P("rows", FEAT), P(FEAT, None), P("rows", None), P())
    return jax.shard_map(
        functools.partial(shards, rows), mesh=torus, in_specs=placed,
        out_specs=P("rows", None, FEAT), check_vma=False,
    )
```

time: 166 us -> 157 us (0.946)
  Pallas kernels: 160 us -> 155 us
  local copies, waits for them, and re-layouts: 4.71 us -> 0.7 us
    unnamed x6 -> x2, local copies, waits for them, and re-layouts: 4.71 us -> 0.7 us
    pallas_call x1, Pallas kernels: 7.89 us -> 4.53 us  [spread_rows(): pl.pallas_call(pack_kernel, out_shape=jax.ShapeDtypeStruct((2 * rows * CA...]
    pallas_call x1, Pallas kernels: 23.3 us -> 21.1 us  [exchange(): pl.pallas_call(functools.partial(exchange_kernel, rows), out_shape=jax.Sh...]
    pallas_call x2, Pallas kernels: 106 us -> 104 us  [covariance(): pl.pallas_call(functools.partial(covariance_kernel, rows, first), out_sha...]
    pallas_call x1, Pallas kernels: 14.2 us -> 16.1 us  [project(): pl.pallas_call(project_kernel, out_shape=jax.ShapeDtypeStruct((length, ha...]
where the time goes in v3:
time: 157 us; the launch traced here: 156 us
  Pallas kernels  155 us (99%)
    pallas_call x2, Pallas kernels, covariance(): pl.pallas_call(functools.partial(covariance_kernel, rows, first), out_sha...  104 us
    pallas_call x1, Pallas kernels, exchange(): pl.pallas_call(functools.partial(exchange_kernel, rows), out_shape=jax.Sh...  21.1 us
    pallas_call x1, Pallas kernels, project(): pl.pallas_call(project_kernel, out_shape=jax.ShapeDtypeStruct((length, ha...  16.1 us
    pallas_call x2, Pallas kernels, new_basis(): pl.pallas_call(functools.partial(basis_kernel, last), out_shape=jax.Shape...  7.61 us
    pallas_call x1, Pallas kernels, spread_rows(): pl.pallas_call(pack_kernel, out_shape=jax.ShapeDtypeStruct((2 * rows * CA...  4.53 us

profile of v3, /device:TPU:0, one launch (start us, length us, event | category | flops | bytes accessed | tf_op | source)
XLA Modules:
  0.0 156.3 jit_solution(6011300604915645930)
XLA Ops:
  0.7 0.0 copy-start
  0.7 0.7 copy-done
  1.4 55.5 %covariance.2 = (bf16[2,32,16,256]{3,2,1,0:T(8,128)(2,1)S(1)}, f32[3,128,128]{2,1,0:T(8,128)S(1)}, s32[24,128]{1,0:T(8,128)S(1)}) custom-call(bf16[3072,1024]{1,0:T(8,128)(2,1)} %source.1, f32[1024,256]{1,0:T(8,128)} %refs_1_.1, s32[24,128]{1,0:T(8,128)S(1)} %bitcast.5), custom_call_target="tpu_custom_call" | custom-call | tf_op jit(solution)/shard_map/covariance/pallas_call | solution.py:307
  56.8 4.1 %new_basis.2.refs_1_ = bf16[1024,256]{1,0:T(8,128)(2,1)S(1)} custom-call(s32[1]{0:T(128)S(6)} %copy.5.kept, f32[3,128,128]{2,1,0:T(8,128)S(1)} %get-tuple-element.11.gram, bf16[2,32,16,256]{3,2,1,0:T(8,128)(2,1)S(1)} %get-tuple-element.12.z), custom_call_target="tpu_custom_call" | custom-call | tf_op jit(solution)/shard_map/new_basis/pallas_call | solution.py:437
  60.9 48.8 %covariance.3 = (bf16[2,32,16,256]{3,2,1,0:T(8,128)(2,1)S(1)}, f32[3,128,128]{2,1,0:T(8,128)S(1)}) custom-call(bf16[3072,1024]{1,0:T(8,128)(2,1)} %source.1, bf16[1024,256]{1,0:T(8,128)(2,1)S(1)} %new_basis.2.refs_1_), custom_call_target="tpu_custom_call" | custom-call | tf_op jit(solution)/shard_map/covariance/pallas_call | solution.py:307
  109.7 3.6 %new_basis.3.q = bf16[1024,256]{1,0:T(8,128)(2,1)S(1)} custom-call(s32[1]{0:T(128)S(6)} %copy.5.kept, f32[3,128,128]{2,1,0:T(8,128)S(1)} %get-tuple-element.13.gram, bf16[2,32,16,256]{3,2,1,0:T(8,128)(2,1)S(1)} %get-tuple-element.14.z), custom_call_target="tpu_custom_call" | custom-call | tf_op jit(solution)/shard_map/new_basis/pallas_call | solution.py:437
  113.3 16.1 %project.1.p = bf16[3072,128]{1,0:T(8,128)(2,1)S(1)} custom-call(bf16[3072,1024]{1,0:T(8,128)(2,1)} %source.1, bf16[1024,256]{1,0:T(8,128)(2,1)S(1)} %new_basis.3.q), custom_call_target="tpu_custom_call" | custom-call | tf_op jit(solution)/shard_map/project/pallas_call | solution.py:519
  129.4 4.5 %spread_rows.1.spread = f32[8192,128]{1,0:T(8,128)S(1)} custom-call(s32[3072]{0:T(1024)S(1)} %bitcast.4, s32[1]{0:T(128)} %bitcast.2.side, bf16[3072,128]{1,0:T(8,128)(2,1)S(1)} %project.1.p), custom_call_target="tpu_custom_call" | custom-call | tf_op jit(solution)/shard_map/spread_rows/pallas_call | solution.py:564
  133.9 21.1 %exchange.1.arrived = bf16[32,128,128]{2,1,0:T(8,128)(2,1)S(1)} custom-call(f32[8192,128]{1,0:T(8,128)S(1)} %spread_rows.1.spread), custom_call_target="tpu_custom_call" | custom-call | tf_op jit(solution)/shard_map/exchange/pallas_call | solution.py:610
  155.0 1.2 arrange.1
Async XLA Ops:
  0.7 0.7 copy-start

commit v4 on v3

--- a/solution.py
+++ b/solution.py
@@ -11,8 +11,8 @@
 ITERS = 2
 CAP = 128
 SHARES = (1, 2, 2, 2, 2, 2, 1)
-NP = 4
-NS = 2
+NS = 1
+GRANT = 44
 TOL = 2e-3
 COARSE = 1.0
 STEPS = 14
@@ -114,10 +114,10 @@
 
 def covariance_kernel(rows, first, *refs):
     if first:
-        source, basis, names, z_out, gram_out, place, q, ids, *refs = refs
+        source, basis, names, z_out, gram_out, place, slab, q, ids, load_sem, *refs = refs
     else:
-        source, q, z_out, gram_out, *refs = refs
-    (slab, load_sem, qb, away, home, part, mine, theirs, y, z, z_send, z_recv, z_full, g_part, g_near, g_mine, g_far, g_all,
+        slab, q, z_out, gram_out, *refs = refs
+    (qb, away, home, part, mine, theirs, y, z, z_send, z_recv, z_full, g_part, g_near, g_mine, g_far, g_all,
      near_sem, far_sem, y_sem, rs_sem, ag_sem, g_sem, round_a, round_b) = refs
     me, core, xl = lax.axis_index("rows"), lax.axis_index("core"), lax.axis_index("xl")
     near, far = {"core": 1 - core}, {"xl": 1 - xl}
@@ -136,10 +136,10 @@
         at = rows_at(core if own else 1 - core, i)
         return pltpu.make_async_copy(source.at[at], slab.at[at], load_sem.at[own, i])
 
-    for i in range(count):
-        load(0, i).start()
-        load(1, i).start()
     if first:
+        for i in range(count):
+            load(0, i).start()
+            load(1, i).start()
         begin = pltpu.make_async_copy(basis, q, load_sem.at[0, count])
         naming = pltpu.make_async_copy(names, ids, load_sem.at[1, count])
         begin.start()
@@ -150,7 +150,8 @@
         return slab[rows_at(core if own else 1 - core, i), :]
 
     def scores(own, i):
-        load(own, i).wait()
+        if first:
+            load(own, i).wait()
         return nn(held(own, i), qb[...])
 
     def at(ref, i):
@@ -298,11 +299,11 @@
     dma = pltpu.SemaphoreType.DMA
     first = ids is not None
     out = [jax.ShapeDtypeStruct((NS, rows, *piece), BF16), jax.ShapeDtypeStruct((3, low, low), F32)]
-    args, extra, specs = [slab, q], [], [HBM, VMEM]
+    args, extra, specs = [slab, q], [], [VMEM, VMEM]
     if first:
-        out.append(jax.ShapeDtypeStruct(ids.shape, jnp.int32))
+        out += [jax.ShapeDtypeStruct(ids.shape, jnp.int32), jax.ShapeDtypeStruct(slab.shape, BF16)]
         args.append(ids)
-        extra = [pltpu.VMEM(q.shape, F32), pltpu.VMEM(ids.shape, jnp.int32)]
+        extra = [pltpu.VMEM(q.shape, F32), pltpu.VMEM(ids.shape, jnp.int32), dma((2, count + 1))]
         specs = [HBM] * 3
     return pl.pallas_call(
         functools.partial(covariance_kernel, rows, first),
@@ -310,8 +311,6 @@
         in_specs=specs,
         out_specs=[VMEM] * len(out),
         scratch_shapes=extra + [
-            pltpu.VMEM(slab.shape, BF16),
-            dma((2, count + 1)),
             pltpu.VMEM(q.shape, BF16),
             pltpu.VMEM((half, width), BF16),
             pltpu.VMEM((half, width), BF16),
@@ -338,7 +337,7 @@
             pltpu.SemaphoreType.REGULAR,
         ],
         compiler_params=pltpu.CompilerParams(
-            collective_id=ident, has_side_effects=True, vmem_limit_bytes=(53 if first else 52) << 20
+            collective_id=ident, has_side_effects=True, vmem_limit_bytes=(GRANT if first else 32) << 20
         ),
         name="covariance",
     )(*args)
@@ -445,98 +444,97 @@
     )(kept, gram, z)
 
 
-def project_kernel(source, q, p_out, slab, away, home, part, keep, send, recv, p,
-                   load_sem, near_sem, far_sem, p_sem):
+def project_kernel(slab, q, p_out, away, home, keep, send, recv, p, near_sem, far_sem, p_sem):
     core, xl = lax.axis_index("core"), lax.axis_index("xl")
     near, far = {"core": 1 - core}, {"xl": 1 - xl}
-    chunk = source.shape[0] // (2 * NP)
-    width = q.shape[1]
-    half = width // 2
+    half_rows = slab.shape[0] // 2
+    half = q.shape[1] // 2
+    chunks = chunks_of(half_rows)
+    count = len(chunks)
     barrier = greet((near, far))
 
-    def load(own, i):
+    def scores(own, i):
+        start, size = chunks[i]
         h = core if own else 1 - core
-        at = pl.ds(pl.multiple_of(h * NP * chunk + i * chunk, chunk), chunk)
-        return pltpu.make_async_copy(source.at[at], slab.at[at], load_sem.at[own, i])
-
-    for i in range(NP):
-        load(0, i).start()
-        load(1, i).start()
-
-    def scores(own, i):
-        load(own, i).wait()
-        h = core if own else 1 - core
-        return nn(slab[pl.ds(pl.multiple_of(h * NP * chunk + i * chunk, chunk), chunk), :], q[...])
+        return nn(slab[pl.ds(pl.multiple_of(h * half_rows + start, 8), size), :], q[...])
+
+    def at(ref, i):
+        start, size = chunks[i]
+        return ref.at[pl.ds(start, size)]
+
+    def p_at(own, i):
+        return at(p.at[core if own else 1 - core], i)
 
     def to_near(i):
-        return remote(away.at[i], home.at[i], near_sem.at[0, i], near_sem.at[1, i], near)
+        return remote(at(away, i), at(home, i), near_sem.at[0, i], near_sem.at[1, i], near)
 
     def to_far(i):
-        return remote(send.at[i], recv.at[i], far_sem.at[0, i], far_sem.at[1, i], far)
+        return remote(at(send, i), at(recv, i), far_sem.at[0, i], far_sem.at[1, i], far)
 
     def share(i):
-        return remote(p.at[core, i], p.at[core, i], p_sem.at[0, i], p_sem.at[1, i], near)
+        return remote(p_at(1, i), p_at(1, i), p_sem.at[0, i], p_sem.at[1, i], near)
 
     def shared(i):
-        return remote(p.at[1 - core, i], p.at[1 - core, i], p_sem.at[0, i], p_sem.at[1, i], near)
-
-    def chip_sum(i):
+        return remote(p_at(0, i), p_at(0, i), p_sem.at[0, i], p_sem.at[1, i], near)
+
+    def chip_sum(i, part):
         to_near(i).wait_recv()
-        both = part[i] + home[i].astype(F32)
+        both = part + at(home, i)[...].astype(F32)
         low, high = both[:, :half], both[:, half:]
-        keep[i] = jnp.where(xl == 0, low, high)
-        send[i] = jnp.where(xl == 0, high, low).astype(BF16)
+        at(send, i)[...] = jnp.where(xl == 0, high, low).astype(BF16)
         to_far(i).start()
-
-    for i in range(NP):
-        away[i] = scores(0, i).astype(BF16)
-        if i == 0:
-            pl.semaphore_wait(barrier, 2)
-        to_near(i).start()
-        part[i] = scores(1, i)
-        if i > 0:
-            chip_sum(i - 1)
-    chip_sum(NP - 1)
-    for i in range(NP):
+        at(keep, i)[...] = jnp.where(xl == 0, low, high)
+
+    for i in range(2):
+        at(away, i)[...] = scores(0, i).astype(BF16)
+    own = [scores(1, 0)]
+    pl.semaphore_wait(barrier, 2)
+    to_near(0).start()
+    to_near(1).start()
+    for i in range(count):
+        if i + 2 < count:
+            at(away, i + 2)[...] = scores(0, i + 2).astype(BF16)
+            to_near(i + 2).start()
+        if i + 1 < count:
+            own.append(scores(1, i + 1))
+        chip_sum(i, own[i])
+    for i in range(count):
         to_far(i).wait_recv()
-        p[core, i] = (keep[i] + recv[i].astype(F32)).astype(BF16)
+        p_at(1, i)[...] = (at(keep, i)[...] + at(recv, i)[...].astype(F32)).astype(BF16)
         share(i).start()
-    for i in range(NP):
+    for i in range(count):
+        to_near(i).wait_send()
+        to_far(i).wait_send()
+    for i in range(count):
         shared(i).wait_recv()
     p_out[...] = p[...].reshape(p_out.shape)
-    for i in range(NP):
-        to_near(i).wait_send()
-        to_far(i).wait_send()
+    for i in range(count):
         share(i).wait_send()
 
 
 def project(slab, q, ident):
     length = slab.shape[0]
     width = q.shape[1]
-    chunk = length // (2 * NP)
     half = width // 2
-    dma = pltpu.SemaphoreType.DMA
+    dma = pltpu.SemaphoreType.DMA((2, len(SHARES)))
     return pl.pallas_call(
         project_kernel,
         out_shape=jax.ShapeDtypeStruct((length, half), BF16),
-        in_specs=[HBM, VMEM],
+        in_specs=[VMEM, VMEM],
         out_specs=VMEM,
         scratch_shapes=[
-            pltpu.VMEM(slab.shape, BF16),
-            pltpu.VMEM((NP, chunk, width), BF16),
-            pltpu.VMEM((NP, chunk, width), BF16),
-            pltpu.VMEM((NP, chunk, width), F32),
-            pltpu.VMEM((NP, chunk, half), F32),
-            pltpu.VMEM((NP, chunk, half), BF16),
-            pltpu.VMEM((NP, chunk, half), BF16),
-            pltpu.VMEM((2, NP, chunk, half), BF16),
-            dma((2, NP)),
-            dma((2, NP)),
-            dma((2, NP)),
-            dma((2, NP)),
+            pltpu.VMEM((length // 2, width), BF16),
+            pltpu.VMEM((length // 2, width), BF16),
+            pltpu.VMEM((length // 2, half), F32),
+            pltpu.VMEM((length // 2, half), BF16),
+            pltpu.VMEM((length // 2, half), BF16),
+            pltpu.VMEM((2, length // 2, half), BF16),
+            dma,
+            dma,
+            dma,
         ],
         compiler_params=pltpu.CompilerParams(
-            collective_id=ident, has_side_effects=True, vmem_limit_bytes=52 << 20
+            collective_id=ident, has_side_effects=True, vmem_limit_bytes=24 << 20
         ),
         name="project",
     )(slab, q)
@@ -645,7 +643,7 @@
 
 def shards(rows, slab, basis, cluster_ids, kept):
     side = jnp.broadcast_to(lax.axis_index("core"), (1,)).astype(jnp.int32)
-    z, gram, place = covariance(slab, basis, rows, 0, cluster_ids.reshape(-1, CAP))
+    z, gram, place, slab = covariance(slab, basis, rows, 0, cluster_ids.reshape(-1, CAP))
     for step in range(1, ITERS):
         q = new_basis(kept, gram, z, False)
         z, gram = covariance(slab, q, rows, step)

time: 157 us -> 154 us (0.981)
  Pallas kernels: 155 us -> 151 us
    pallas_call x2, Pallas kernels: 104 us -> 102 us  [covariance(): pl.pallas_call(functools.partial(covariance_kernel, rows, first), out_sha...]
    pallas_call x1, Pallas kernels: 16.1 us -> 14.3 us  [project(): pl.pallas_call(project_kernel, out_shape=jax.ShapeDtypeStruct((length, ha...]
where the time goes in v4:
time: 154 us; the launch traced here: 153 us
  Pallas kernels  151 us (98%)
  local copies, waits for them, and re-layouts  1.93 us (1%)
    pallas_call x2, Pallas kernels, covariance(): pl.pallas_call(functools.partial(covariance_kernel, rows, first), out_sha...  102 us
    pallas_call x1, Pallas kernels, exchange(): pl.pallas_call(functools.partial(exchange_kernel, rows), out_shape=jax.Sh...  20.8 us
    pallas_call x1, Pallas kernels, project(): pl.pallas_call(project_kernel, out_shape=jax.ShapeDtypeStruct((length, ha...  14.3 us
    pallas_call x2, Pallas kernels, new_basis(): pl.pallas_call(functools.partial(basis_kernel, last), out_shape=jax.Shape...  7.55 us
    pallas_call x1, Pallas kernels, spread_rows(): pl.pallas_call(pack_kernel, out_shape=jax.ShapeDtypeStruct((2 * rows * CA...  4.53 us

profile of v4, /device:TPU:0, one launch (start us, length us, event | category | flops | bytes accessed | tf_op | source)
XLA Modules:
  0.0 153.2 jit_solution(3780434907212448029)
XLA Ops:
  0.0 0.0 copy-start
  0.0 1.2 copy-done
  1.2 0.0 copy-start.1
  1.2 0.7 copy-done.1
  1.9 52.6 %covariance.2 = (bf16[1,32,16,512]{3,2,1,0:T(8,128)(2,1)S(1)}, f32[3,128,128]{2,1,0:T(8,128)S(1)}, s32[24,128]{1,0:T(8,128)S(1)}, bf16[3072,1024]{1,0:T(8,128)(2,1)S(1)}) custom-call(bf16[3072,1024]{1,0:T(8,128)(2,1)} %refs_0_.1, f32[1024,256]{1,0:T(8,128)S(1)} %copy-done, s32[24,128]{1,0:T(8,128)S(1)} %bitcast.5), custom_call_target="tpu_custom_call" | custom-call | tf_op jit(solution)/shard_map/covariance/pallas_call | solution.py:308
  55.1 4.0 %new_basis.2.refs_1_ = bf16[1024,256]{1,0:T(8,128)(2,1)S(1)} custom-call(s32[1]{0:T(128)S(6)} %copy.5.kept, f32[3,128,128]{2,1,0:T(8,128)S(1)} %get-tuple-element.13.gram, bf16[1,32,16,512]{3,2,1,0:T(8,128)(2,1)S(1)} %get-tuple-element.14.z), custom_call_target="tpu_custom_call" | custom-call | tf_op jit(solution)/shard_map/new_basis/pallas_call | solution.py:436
  59.2 49.6 %covariance.3 = (bf16[1,32,16,512]{3,2,1,0:T(8,128)(2,1)S(1)}, f32[3,128,128]{2,1,0:T(8,128)S(1)}) custom-call(bf16[3072,1024]{1,0:T(8,128)(2,1)S(1)} %get-tuple-element.12.refs_0_.slab, bf16[1024,256]{1,0:T(8,128)(2,1)S(1)} %new_basis.2.refs_1_), custom_call_target="tpu_custom_call" | custom-call | tf_op jit(solution)/shard_map/covariance/pallas_call | solution.py:308
  108.8 3.5 %new_basis.3.q = bf16[1024,256]{1,0:T(8,128)(2,1)S(1)} custom-call(s32[1]{0:T(128)S(6)} %copy.5.kept, f32[3,128,128]{2,1,0:T(8,128)S(1)} %get-tuple-element.15.gram, bf16[1,32,16,512]{3,2,1,0:T(8,128)(2,1)S(1)} %get-tuple-element.16.z), custom_call_target="tpu_custom_call" | custom-call | tf_op jit(solution)/shard_map/new_basis/pallas_call | solution.py:436
  112.3 14.3 %project.1.p = bf16[3072,128]{1,0:T(8,128)(2,1)S(1)} custom-call(bf16[3072,1024]{1,0:T(8,128)(2,1)S(1)} %get-tuple-element.12.refs_0_.slab, bf16[1024,256]{1,0:T(8,128)(2,1)S(1)} %new_basis.3.q), custom_call_target="tpu_custom_call" | custom-call | tf_op jit(solution)/shard_map/project/pallas_call | solution.py:520
  126.6 4.5 %spread_rows.1.spread = f32[8192,128]{1,0:T(8,128)S(1)} custom-call(s32[3072]{0:T(1024)S(1)} %bitcast.4, s32[1]{0:T(128)} %bitcast.2.side, bf16[3072,128]{1,0:T(8,128)(2,1)S(1)} %project.1.p), custom_call_target="tpu_custom_call" | custom-call | tf_op jit(solution)/shard_map/spread_rows/pallas_call | solution.py:562
  131.2 20.8 %exchange.1.arrived = bf16[32,128,128]{2,1,0:T(8,128)(2,1)S(1)} custom-call(f32[8192,128]{1,0:T(8,128)S(1)} %spread_rows.1.spread), custom_call_target="tpu_custom_call" | custom-call | tf_op jit(solution)/shard_map/exchange/pallas_call | solution.py:608
  152.0 1.2 arrange.1
Async XLA Ops:
  0.0 1.2 copy-start
  1.2 0.7 copy-start.1

commit v5 on v4

--- a/solution.py
+++ b/solution.py
@@ -112,9 +112,12 @@
         seen = seen + jnp.sum(hot, axis=1, keepdims=True)
 
 
-def covariance_kernel(rows, first, *refs):
+def covariance_kernel(rows, kind, *refs):
+    first, joint = kind == "first", kind == "joint"
     if first:
-        source, basis, names, z_out, gram_out, place, slab, q, ids, load_sem, *refs = refs
+        source, basis, names, z_out, place, slab, q, ids, load_sem, *refs = refs
+    elif joint:
+        slab, z_in, z_out, gram_out, gram_in, size_out, unit, *refs = refs
     else:
         slab, q, z_out, gram_out, *refs = refs
     (qb, away, home, part, mine, theirs, y, z, z_send, z_recv, z_full, g_part, g_near, g_mine, g_far, g_all,
@@ -122,9 +125,13 @@
     me, core, xl = lax.axis_index("rows"), lax.axis_index("core"), lax.axis_index("xl")
     near, far = {"core": 1 - core}, {"xl": 1 - xl}
     half_rows = slab.shape[0] // 2
-    width = q.shape[1]
+    width = qb.shape[1]
     chunks = chunks_of(half_rows)
     count = len(chunks)
+    deep, wide = z_send.shape[2:]
+    group = rows // 2
+    low = width // 2
+    part_rows = low // 2
     beside = axis_peers(me, rows)
     barrier = greet([near, far] + beside)
 
@@ -182,7 +189,52 @@
         for peer in beside:
             pl.semaphore_signal(sem, inc=1, device_id=peer, device_id_type=MESH)
 
-    qb[...] = q[...].astype(BF16)
+    def gram_terms(e, pieces, s):
+        for f in range(2):
+            block = pieces[s, f * group:(f + 1) * group].reshape(width, wide)
+            terms_of = (nt(block[:low], block[:low]), nt(block[low:], block[:low]), nt(block[low:], block[low:]))
+            for b, term in enumerate(terms_of):
+                for h in range(2):
+                    line = term[h * part_rows:(h + 1) * part_rows]
+                    g_part[e, h, b] = line if s + f == 0 else g_part[e, h, b] + line
+
+    def gram_copy(e, i, src, dst, target):
+        return remote(src, dst, g_sem.at[0, e, i], g_sem.at[1, e, i], target)
+
+    def gram_near(e):
+        return gram_copy(e, 0, g_part.at[e, 1 - core], g_near.at[e], near)
+
+    def gram_far(e):
+        return gram_copy(e, 1, g_mine.at[e], g_far.at[e], far)
+
+    def gram_back(e, c):
+        return gram_copy(e, 2, g_all.at[e, c], g_all.at[e, c], near)
+
+    def gram_to_far(e):
+        gram_near(e).wait_recv()
+        g_mine[e] = g_part[e, core] + g_near[e]
+        gram_far(e).start()
+
+    def gram_finish(e, out):
+        gram_far(e).wait_recv()
+        g_all[e, core] = g_mine[e] + g_far[e]
+        gram_back(e, core).start()
+        gram_back(e, 1 - core).wait_recv()
+        for h in range(2):
+            for b in range(3):
+                out[b, h * part_rows:(h + 1) * part_rows, :] = g_all[e, h, b]
+        gram_near(e).wait_send()
+        gram_far(e).wait_send()
+        gram_back(e, core).wait_send()
+
+    if joint:
+        for s in range(NS):
+            gram_terms(1, z_in, s)
+            for f in range(2):
+                left = (f * NS + s) * wide
+                qb[left:left + wide, :] = z_in[s, f * group:(f + 1) * group].reshape(width, wide).T
+    else:
+        qb[...] = q[...].astype(BF16)
     for i in range(count):
         at(away, i)[...] = scores(0, i).astype(BF16)
         if i == 0:
@@ -190,9 +242,13 @@
             continue
         if i == 1:
             pl.semaphore_wait(barrier, len(beside) + 2)
+            if joint:
+                gram_near(1).start()
             to_near(0).start()
         to_near(i).start()
         at(part, i)[...] = scores(1, i)
+        if joint and i == 1:
+            gram_to_far(1)
         chip_sum(i - 1)
         if i == 2:
             pass_on(round_a)
@@ -203,6 +259,11 @@
         naming.wait()
         find_places(2 * rows, ids, place)
     pl.semaphore_wait(round_b, len(beside))
+    if joint:
+        gram_finish(1, gram_in)
+        inverse, last_size = steps_for(gram_in, unit)
+        top, rest = split(inverse)
+        size_out[...] = jnp.full(size_out.shape, last_size)
 
     def add(own, i, start=False):
         term = tn(y_at(own, i)[...], held(own, i))
@@ -210,7 +271,8 @@
 
     for i in range(count):
         to_far(i).wait_recv()
-        y_at(1, i)[...] = (at(mine, i)[...].astype(F32) + at(theirs, i)[...].astype(F32)).astype(BF16)
+        both = (at(mine, i)[...].astype(F32) + at(theirs, i)[...].astype(F32)).astype(BF16)
+        y_at(1, i)[...] = (nt(both, top) + nt(both, rest)).astype(BF16) if joint else both
         share(i).start()
         add(1, i, i == 0)
         if i > 0:
@@ -219,8 +281,6 @@
     shared(count - 1).wait_recv()
     add(0, count - 1)
 
-    deep, wide = z_send.shape[2:]
-    group = rows // 2
     peers = peers_of(me, rows)
 
     def scatter(s, slot, there):
@@ -247,27 +307,16 @@
         for slot, there, _ in peers:
             gather(s, slot, me, there).start()
 
-    low = width // 2
-    part_rows = low // 2
     for s in range(NS):
         for slot, there, back in reversed(peers):
             gather(s, slot, back, there).wait_recv()
-        for f in range(2):
-            block = z_full[s, f * group:(f + 1) * group].reshape(width, wide)
-            terms_of = (nt(block[:low], block[:low]), nt(block[low:], block[:low]), nt(block[low:], block[low:]))
-            for b, term in enumerate(terms_of):
-                for h in range(2):
-                    line = term[h * part_rows:(h + 1) * part_rows]
-                    g_part[h, b] = line if s + f == 0 else g_part[h, b] + line
-    out_near = remote(g_part.at[1 - core], g_near, g_sem.at[0, 0], g_sem.at[1, 0], near)
-    out_far = remote(g_mine, g_far, g_sem.at[0, 1], g_sem.at[1, 1], far)
-    out_back = remote(g_all.at[core], g_all.at[core], g_sem.at[0, 2], g_sem.at[1, 2], near)
-    in_back = remote(g_all.at[1 - core], g_all.at[1 - core], g_sem.at[0, 2], g_sem.at[1, 2], near)
-    out_near.start()
+        if not first:
+            gram_terms(0, z_full, s)
+    if not first:
+        gram_near(0).start()
     z_out[...] = z_full[...]
-    out_near.wait_recv()
-    g_mine[...] = g_part[core] + g_near[...]
-    out_far.start()
+    if not first:
+        gram_to_far(0)
     for i in range(count):
         to_near(i).wait_send()
         to_far(i).wait_send()
@@ -276,21 +325,14 @@
         for slot, there, _ in peers:
             scatter(s, slot, there).wait_send()
             gather(s, slot, me, there).wait_send()
-    out_far.wait_recv()
-    g_all[core] = g_mine[...] + g_far[...]
-    out_back.start()
-    in_back.wait_recv()
-    for h in range(2):
-        for b in range(3):
-            gram_out[b, h * part_rows:(h + 1) * part_rows, :] = g_all[h, b]
-    out_near.wait_send()
-    out_far.wait_send()
-    out_back.wait_send()
+    if not first:
+        gram_finish(0, gram_out)
 
 
 def covariance(slab, q, rows, ident, ids=None):
+    joint = q.ndim == 4
     length, feats = slab.shape
-    width = q.shape[1]
+    width = q.shape[1] * q.shape[2] // 2 if joint else q.shape[1]
     half = length // 2
     count = len(SHARES)
     piece = (2 * width // rows, feats // (2 * NS))
@@ -298,20 +340,26 @@
     parts = (3, low // 2, low)
     dma = pltpu.SemaphoreType.DMA
     first = ids is not None
-    out = [jax.ShapeDtypeStruct((NS, rows, *piece), BF16), jax.ShapeDtypeStruct((3, low, low), F32)]
+    lower = jax.ShapeDtypeStruct((3, low, low), F32)
+    out = [jax.ShapeDtypeStruct((NS, rows, *piece), BF16)] + [lower] * (not first)
     args, extra, specs = [slab, q], [], [VMEM, VMEM]
     if first:
         out += [jax.ShapeDtypeStruct(ids.shape, jnp.int32), jax.ShapeDtypeStruct(slab.shape, BF16)]
         args.append(ids)
         extra = [pltpu.VMEM(q.shape, F32), pltpu.VMEM(ids.shape, jnp.int32), dma((2, count + 1))]
         specs = [HBM] * 3
+    if joint:
+        out += [lower, jax.ShapeDtypeStruct((8, 128), F32)]
+        extra = [pltpu.VMEM((width, width), F32)]
+    kind = "first" if first else "joint" if joint else "plain"
+    grams = 1 + joint
     return pl.pallas_call(
-        functools.partial(covariance_kernel, rows, first),
+        functools.partial(covariance_kernel, rows, kind),
         out_shape=out,
         in_specs=specs,
         out_specs=[VMEM] * len(out),
         scratch_shapes=extra + [
-            pltpu.VMEM(q.shape, BF16),
+            pltpu.VMEM((feats, width), BF16),
             pltpu.VMEM((half, width), BF16),
             pltpu.VMEM((half, width), BF16),
             pltpu.VMEM((half, width), F32),
@@ -322,17 +370,17 @@
             pltpu.VMEM((NS, rows, *piece), BF16),
             pltpu.VMEM((NS, rows, *piece), BF16),
             pltpu.VMEM((NS, rows, *piece), BF16),
-            pltpu.VMEM((2, *parts), F32),
-            pltpu.VMEM(parts, F32),
-            pltpu.VMEM(parts, F32),
-            pltpu.VMEM(parts, F32),
-            pltpu.VMEM((2, *parts), F32),
+            pltpu.VMEM((grams, 2, *parts), F32),
+            pltpu.VMEM((grams, *parts), F32),
+            pltpu.VMEM((grams, *parts), F32),
+            pltpu.VMEM((grams, *parts), F32),
+            pltpu.VMEM((grams, 2, *parts), F32),
             dma((2, count)),
             dma((2, count)),
             dma((2, count)),
             dma((2, NS, rows)),
             dma((2, NS, rows)),
-            dma((2, 3)),
+            dma((2, grams, 3)),
             pltpu.SemaphoreType.REGULAR,
             pltpu.SemaphoreType.REGULAR,
         ],
@@ -353,23 +401,58 @@
     return dot(a0, b0) + (dot(a0, b1) + dot(a1, b0))
 
 
-def basis_kernel(last, kept, gram, z, q_out, unit, x, e, a, state):
-    low = gram.shape[1]
-    n = 2 * low
+def masks(n):
     row = lax.broadcasted_iota(jnp.int32, (n, n), 0)
     col = lax.broadcasted_iota(jnp.int32, (n, n), 1)
-    lower = jnp.where(row > col, F32(1), jnp.where(row == col, F32(0.5), F32(0)))
     eye = jnp.where(row == col, F32(1), F32(0))
-
-    x[:low, :low] = gram[0]
-    x[low:, :low] = gram[1]
-    x[low:, low:] = gram[2]
-    x[:low, low:] = gram[1].T
-    g = x[...]
+    return row, col, eye, jnp.where(row > col, F32(1), F32(0.5) * eye)
+
+
+def whole_gram(gram, out):
+    low = gram.shape[1]
+    out[:low, :low] = gram[0]
+    out[low:, :low] = gram[1]
+    out[low:, low:] = gram[2]
+    out[:low, low:] = gram[1].T
+    return out[...]
+
+
+def unit_diagonal(g, eye):
     diag = g * eye
     across = lax.rsqrt(jnp.sum(diag, axis=0, keepdims=True))
     down = lax.rsqrt(jnp.sum(diag, axis=1, keepdims=True))
-    scaled = g * across * down
+    return g * across * down, across
+
+
+def coarse_residual(x, unit, eye):
+    near = x.astype(BF16)
+    return nt(nn(near, unit.astype(BF16)).astype(BF16), near) - eye
+
+
+def fine_residual(x, unit, eye):
+    return fine(nt, fine(nn, x, unit), x) - eye
+
+
+def improved(x, e, lower):
+    return x - nn((e * lower).astype(BF16), x.astype(BF16))
+
+
+def steps_for(gram, unit):
+    n = unit.shape[0]
+    _, _, eye, lower = masks(n)
+    scaled, across = unit_diagonal(whole_gram(gram, unit), eye)
+    unit[...] = scaled
+    x = eye - (scaled - eye) * lower
+    for step in range(5):
+        e = (coarse_residual if step < 2 else fine_residual)(x, unit[...], eye)
+        x = improved(x, e, lower)
+    return x * across, jnp.sum(e * e)
+
+
+def basis_kernel(last, kept, gram, z, q_out, unit, x, e, a, state):
+    n = unit.shape[0]
+    row, col, eye, lower = masks(n)
+    scaled, across = unit_diagonal(whole_gram(gram, x), eye)
     unit[...] = scaled
     begin = scaled - eye
     e[...] = begin
@@ -382,19 +465,18 @@
         def _():
             now = e[...]
             size = jnp.sum(now * now)
-            better = x[...] - nn((now * lower).astype(BF16), x[...].astype(BF16))
+            better = improved(x[...], now, lower)
             x[...] = better
             done = size < TOL * TOL
             state[0] = done.astype(jnp.int32)
 
             @pl.when(size > COARSE * COARSE)
             def _():
-                near = better.astype(BF16)
-                e[...] = nt(nn(near, unit[...].astype(BF16)).astype(BF16), near) - eye
+                e[...] = coarse_residual(better, unit[...], eye)
 
             @pl.when(jnp.logical_not(done) & jnp.logical_not(size > COARSE * COARSE))
             def _():
-                e[...] = fine(nt, fine(nn, better, unit[...]), better) - eye
+                e[...] = fine_residual(better, unit[...], eye)
 
     @pl.when(state[0] == 0)
     def _():
@@ -444,7 +526,7 @@
     )(kept, gram, z)
 
 
-def project_kernel(slab, q, p_out, away, home, keep, send, recv, p, near_sem, far_sem, p_sem):
+def project_kernel(source, q, p_out, slab, away, home, keep, send, recv, p, near_sem, far_sem, p_sem, load_sem):
     core, xl = lax.axis_index("core"), lax.axis_index("xl")
     near, far = {"core": 1 - core}, {"xl": 1 - xl}
     half_rows = slab.shape[0] // 2
@@ -453,10 +535,22 @@
     count = len(chunks)
     barrier = greet((near, far))
 
-    def scores(own, i):
+    def rows_at(own, i):
         start, size = chunks[i]
         h = core if own else 1 - core
-        return nn(slab[pl.ds(pl.multiple_of(h * half_rows + start, 8), size), :], q[...])
+        return pl.ds(pl.multiple_of(h * half_rows + start, 8), size)
+
+    def load(own, i):
+        at = rows_at(own, i)
+        return pltpu.make_async_copy(source.at[at], slab.at[at], load_sem.at[own, i])
+
+    for i in range(count):
+        load(0, i).start()
+        load(1, i).start()
+
+    def scores(own, i):
+        load(own, i).wait()
+        return nn(slab[rows_at(own, i), :], q[...])
 
     def at(ref, i):
         start, size = chunks[i]
@@ -520,9 +614,10 @@
     return pl.pallas_call(
         project_kernel,
         out_shape=jax.ShapeDtypeStruct((length, half), BF16),
-        in_specs=[VMEM, VMEM],
+        in_specs=[HBM, VMEM],
         out_specs=VMEM,
         scratch_shapes=[
+            pltpu.VMEM(slab.shape, BF16),
             pltpu.VMEM((length // 2, width), BF16),
             pltpu.VMEM((length // 2, width), BF16),
             pltpu.VMEM((length // 2, half), F32),
@@ -532,9 +627,10 @@
             dma,
             dma,
             dma,
+            dma,
         ],
         compiler_params=pltpu.CompilerParams(
-            collective_id=ident, has_side_effects=True, vmem_limit_bytes=24 << 20
+            collective_id=ident, has_side_effects=True, vmem_limit_bytes=32 << 20
         ),
         name="project",
     )(slab, q)
@@ -643,10 +739,17 @@
 
 def shards(rows, slab, basis, cluster_ids, kept):
     side = jnp.broadcast_to(lax.axis_index("core"), (1,)).astype(jnp.int32)
-    z, gram, place, slab = covariance(slab, basis, rows, 0, cluster_ids.reshape(-1, CAP))
+    z, place, near_slab = covariance(slab, basis, rows, 0, cluster_ids.reshape(-1, CAP))
     for step in range(1, ITERS):
-        q = new_basis(kept, gram, z, False)
-        z, gram = covariance(slab, q, rows, step)
+        after, gram, before, size = covariance(near_slab, z, rows, step)
+
+        def again(before, z, after, gram):
+            return tuple(covariance(slab, new_basis(kept, before, z, False), rows, ITERS + 1 + step))
+
+        def kept_on(before, z, after, gram):
+            return after, gram
+
+        z, gram = lax.cond(size[0, 0] < TOL * TOL, kept_on, again, before, z, after, gram)
     q = new_basis(kept, gram, z, True)
     p = project(slab, q, ITERS)
     spread = spread_rows(place.reshape(-1), side, p, rows)

time: 154 us -> 148 us (0.961)
  Pallas kernels: 151 us -> 144 us
    pallas_call x2 -> x1, Pallas kernels: 7.55 us -> 3.52 us  [new_basis(): pl.pallas_call(functools.partial(basis_kernel, last), out_shape=jax.Shape...]
    pallas_call x2, Pallas kernels: 102 us -> 98.4 us  [covariance(): pl.pallas_call(functools.partial(covariance_kernel, rows, kind), out_shap...]
where the time goes in v5:
time: 148 us
  Pallas kernels  144 us (97%)
  local copies, waits for them, and re-layouts  2.45 us (2%)
    pallas_call x2, Pallas kernels, covariance(): pl.pallas_call(functools.partial(covariance_kernel, rows, kind), out_shap...  98.4 us
    pallas_call x1, Pallas kernels, exchange(): pl.pallas_call(functools.partial(exchange_kernel, rows), out_shape=jax.Sh...  21.5 us
    pallas_call x1, Pallas kernels, project(): pl.pallas_call(project_kernel, out_shape=jax.ShapeDtypeStruct((length, ha...  15 us
    pallas_call x1, Pallas kernels, spread_rows(): pl.pallas_call(pack_kernel, out_shape=jax.ShapeDtypeStruct((2 * rows * CA...  4.53 us
    pallas_call x1, Pallas kernels, new_basis(): pl.pallas_call(functools.partial(basis_kernel, last), out_shape=jax.Shape...  3.52 us

profile of v5, /device:TPU:0, one launch (start us, length us, event | category | flops | bytes accessed | tf_op | source)
XLA Modules:
  0.0 148.0 jit_solution(5289902008249974788)
XLA Ops:
  0.0 0.0 copy-start
  0.0 1.2 copy-done
  1.2 0.0 copy-start.1
  1.2 0.7 copy-done.1
  1.9 0.0 copy-start.2
  1.9 47.9 %covariance.4 = (bf16[1,32,16,512]{3,2,1,0:T(8,128)(2,1)S(1)}, s32[24,128]{1,0:T(8,128)S(1)}, bf16[3072,1024]{1,0:T(8,128)(2,1)S(1)}) custom-call(bf16[3072,1024]{1,0:T(8,128)(2,1)} %source.1, f32[1024,256]{1,0:T(8,128)S(1)} %copy-done, s32[24,128]{1,0:T(8,128)S(1)} %bitcast.6), custom_call_target="tpu_custom_call" | custom-call | tf_op jit(solution)/shard_map/covariance/pallas_call | solution.py:356
  49.9 50.5 %covariance.5 = (bf16[1,32,16,512]{3,2,1,0:T(8,128)(2,1)S(1)}, f32[3,128,128]{2,1,0:T(8,128)S(1)}, f32[3,128,128]{2,1,0:T(8,128)S(1)}, f32[8,128]{1,0:T(8,128)S(1)}) custom-call(bf16[3072,1024]{1,0:T(8,128)(2,1)S(1)} %get-tuple-element.31.refs_0_, bf16[1,32,16,512]{3,2,1,0:T(8,128)(2,1)S(1)} %get-tuple-element.32.refs_1_), custom_call_target="tpu_custom_call" | custom-call | tf_op jit(solution)/shard_map/covariance/pallas_call | solution.py:356
  100.4 0.5 slice.3
  101.6 0.0 copy-done.2
  102.2 3.5 %new_basis.3.q = bf16[1024,256]{1,0:T(8,128)(2,1)S(1)} custom-call(s32[1]{0:T(128)S(6)} %copy.9.kept, f32[3,128,128]{2,1,0:T(8,128)S(1)} %get-tuple-element.37.gram, bf16[1,32,16,512]{3,2,1,0:T(8,128)(2,1)S(1)} %get-tuple-element.38.z), custom_call_target="tpu_custom_call" | custom-call | tf_op jit(solution)/shard_map/new_basis/pallas_call | solution.py:518
  105.8 15.0 %project.1.p = bf16[3072,128]{1,0:T(8,128)(2,1)S(1)} custom-call(bf16[3072,1024]{1,0:T(8,128)(2,1)} %source.1, bf16[1024,256]{1,0:T(8,128)(2,1)S(1)} %new_basis.3.q), custom_call_target="tpu_custom_call" | custom-call | tf_op jit(solution)/shard_map/project/pallas_call | solution.py:614
  120.8 4.5 %spread_rows.1.spread = f32[8192,128]{1,0:T(8,128)S(1)} custom-call(s32[3072]{0:T(1024)S(1)} %bitcast.5, s32[1]{0:T(128)} %bitcast.2.side, bf16[3072,128]{1,0:T(8,128)(2,1)S(1)} %project.1.p), custom_call_target="tpu_custom_call" | custom-call | tf_op jit(solution)/shard_map/spread_rows/pallas_call | solution.py:658
  125.3 21.5 %exchange.1.arrived = bf16[32,128,128]{2,1,0:T(8,128)(2,1)S(1)} custom-call(f32[8192,128]{1,0:T(8,128)S(1)} %spread_rows.1.spread), custom_call_target="tpu_custom_call" | custom-call | tf_op jit(solution)/shard_map/exchange/pallas_call | solution.py:704
  146.8 1.2 arrange.1
  (1 shorter events, 0.0 us)
Async XLA Ops:
  0.0 1.2 copy-start
  1.2 0.7 copy-start.1
  1.9 99.6 %copy-start.2 = (bf16[3072,1024]{1,0:T(8,128)(2,1)S(1)}, bf16[3072,1024]{1,0:T(8,128)(2,1)}, u32[]{:S(2)}) copy-start(bf16[3072,1024]{1,0:T(8,128)(2,1)} %source.1) | copy-start | bytes 18874372

commit v6 on v5

--- a/solution.py
+++ b/solution.py
@@ -69,9 +69,9 @@
         return sorted(range(n), key=lambda d: -min(d, n - d))
 
     found = []
-    for dz in order(len(lists[0])):
-        for dy in order(len(lists[1])):
-            for dx in order(len(lists[2])):
+    for dx in order(len(lists[2])):
+        for dz in order(len(lists[0])):
+            for dy in order(len(lists[1])):
                 if dz or dy or dx:
                     there = lists[0][dz] + lists[1][dy] + lists[2][dx]
                     back = lists[0][-dz] + lists[1][-dy] + lists[2][-dx]
@@ -115,7 +115,7 @@
 def covariance_kernel(rows, kind, *refs):
     first, joint = kind == "first", kind == "joint"
     if first:
-        source, basis, names, z_out, place, slab, q, ids, load_sem, *refs = refs
+        source, basis, z_out, slab, q, load_sem, *refs = refs
     elif joint:
         slab, z_in, z_out, gram_out, gram_in, size_out, unit, *refs = refs
     else:
@@ -148,9 +148,7 @@
             load(0, i).start()
             load(1, i).start()
         begin = pltpu.make_async_copy(basis, q, load_sem.at[0, count])
-        naming = pltpu.make_async_copy(names, ids, load_sem.at[1, count])
         begin.start()
-        naming.start()
         begin.wait()
 
     def held(own, i):
@@ -255,15 +253,12 @@
     chip_sum(count - 1)
     pl.semaphore_wait(round_a, len(beside))
     pass_on(round_b)
-    if first:
-        naming.wait()
-        find_places(2 * rows, ids, place)
     pl.semaphore_wait(round_b, len(beside))
     if joint:
         gram_finish(1, gram_in)
         inverse, last_size = steps_for(gram_in, unit)
         top, rest = split(inverse)
-        size_out[...] = jnp.full(size_out.shape, last_size)
+        size_out[0, 0] = last_size
 
     def add(own, i, start=False):
         term = tn(y_at(own, i)[...], held(own, i))
@@ -329,7 +324,7 @@
         gram_finish(0, gram_out)
 
 
-def covariance(slab, q, rows, ident, ids=None):
+def covariance(slab, q, rows, ident, first=False):
     joint = q.ndim == 4
     length, feats = slab.shape
     width = q.shape[1] * q.shape[2] // 2 if joint else q.shape[1]
@@ -339,17 +334,15 @@
     low = width // 2
     parts = (3, low // 2, low)
     dma = pltpu.SemaphoreType.DMA
-    first = ids is not None
     lower = jax.ShapeDtypeStruct((3, low, low), F32)
     out = [jax.ShapeDtypeStruct((NS, rows, *piece), BF16)] + [lower] * (not first)
     args, extra, specs = [slab, q], [], [VMEM, VMEM]
     if first:
-        out += [jax.ShapeDtypeStruct(ids.shape, jnp.int32), jax.ShapeDtypeStruct(slab.shape, BF16)]
-        args.append(ids)
-        extra = [pltpu.VMEM(q.shape, F32), pltpu.VMEM(ids.shape, jnp.int32), dma((2, count + 1))]
-        specs = [HBM] * 3
+        out.append(jax.ShapeDtypeStruct(slab.shape, BF16))
+        extra = [pltpu.VMEM(q.shape, F32), dma((2, count + 1))]
+        specs = [HBM, HBM]
     if joint:
-        out += [lower, jax.ShapeDtypeStruct((8, 128), F32)]
+        out += [lower, jax.ShapeDtypeStruct((1, 1), F32)]
         extra = [pltpu.VMEM((width, width), F32)]
     kind = "first" if first else "joint" if joint else "plain"
     grams = 1 + joint
@@ -357,7 +350,7 @@
         functools.partial(covariance_kernel, rows, kind),
         out_shape=out,
         in_specs=specs,
-        out_specs=[VMEM] * len(out),
+        out_specs=[SMEM if shape.shape == (1, 1) else VMEM for shape in out],
         scratch_shapes=extra + [
             pltpu.VMEM((feats, width), BF16),
             pltpu.VMEM((half, width), BF16),
@@ -526,7 +519,7 @@
     )(kept, gram, z)
 
 
-def project_kernel(source, q, p_out, slab, away, home, keep, send, recv, p, near_sem, far_sem, p_sem, load_sem):
+def project_kernel(clusters, source, q, ids, p_out, place, slab, away, home, keep, send, recv, p, near_sem, far_sem, p_sem, load_sem):
     core, xl = lax.axis_index("core"), lax.axis_index("xl")
     near, far = {"core": 1 - core}, {"xl": 1 - xl}
     half_rows = slab.shape[0] // 2
@@ -592,6 +585,7 @@
         if i + 1 < count:
             own.append(scores(1, i + 1))
         chip_sum(i, own[i])
+    find_places(clusters, ids, place)
     for i in range(count):
         to_far(i).wait_recv()
         p_at(1, i)[...] = (at(keep, i)[...] + at(recv, i)[...].astype(F32)).astype(BF16)
@@ -606,16 +600,16 @@
         share(i).wait_send()
 
 
-def project(slab, q, ident):
+def project(slab, q, ids, clusters, ident):
     length = slab.shape[0]
     width = q.shape[1]
     half = width // 2
     dma = pltpu.SemaphoreType.DMA((2, len(SHARES)))
     return pl.pallas_call(
-        project_kernel,
-        out_shape=jax.ShapeDtypeStruct((length, half), BF16),
-        in_specs=[HBM, VMEM],
-        out_specs=VMEM,
+        functools.partial(project_kernel, clusters),
+        out_shape=[jax.ShapeDtypeStruct((length, half), BF16), jax.ShapeDtypeStruct(ids.shape, jnp.int32)],
+        in_specs=[HBM, VMEM, VMEM],
+        out_specs=[VMEM, VMEM],
         scratch_shapes=[
             pltpu.VMEM(slab.shape, BF16),
             pltpu.VMEM((length // 2, width), BF16),
@@ -633,7 +627,7 @@
             collective_id=ident, has_side_effects=True, vmem_limit_bytes=32 << 20
         ),
         name="project",
-    )(slab, q)
+    )(slab, q, ids)
 
 
 def pack_kernel(place, side, p, spread, doubled):
@@ -682,13 +676,10 @@
     def send(slot, there, at):
         return remote(buf.at[slot], arrived.at[at], sem.at[0, slot], sem.at[1, slot], {"rows": there})
 
-    ahead = min(12, rows - 1)
-    for slot, there, _ in peers[:ahead]:
+    for slot, there, _ in peers:
         buf[slot] = block(there)
     pl.semaphore_wait(barrier, rows - 1)
     for slot, there, _ in peers:
-        if slot >= ahead:
-            buf[slot] = block(there)
         send(slot, there, me).start()
     out[me] = block(me)
     for slot, there, back in reversed(peers):
@@ -739,7 +730,7 @@
 
 def shards(rows, slab, basis, cluster_ids, kept):
     side = jnp.broadcast_to(lax.axis_index("core"), (1,)).astype(jnp.int32)
-    z, place, near_slab = covariance(slab, basis, rows, 0, cluster_ids.reshape(-1, CAP))
+    z, near_slab = covariance(slab, basis, rows, 0, True)
     for step in range(1, ITERS):
         after, gram, before, size = covariance(near_slab, z, rows, step)
 
@@ -751,7 +742,7 @@
 
         z, gram = lax.cond(size[0, 0] < TOL * TOL, kept_on, again, before, z, after, gram)
     q = new_basis(kept, gram, z, True)
-    p = project(slab, q, ITERS)
+    p, place = project(slab, q, cluster_ids.reshape(-1, CAP), 2 * rows, ITERS)
     spread = spread_rows(place.reshape(-1), side, p, rows)
     return jnp.swapaxes(arrange(exchange(spread, rows, ITERS + 1)), 1, 2)
 

time: 148 us -> 147 us (level)
  no operation moved by 1% of the time
where the time goes in v6:
time: 147 us
  Pallas kernels  145 us (99%)
    pallas_call x2, Pallas kernels, covariance(): pl.pallas_call(functools.partial(covariance_kernel, rows, kind), out_shap...  99 us
    pallas_call x1, Pallas kernels, exchange(): pl.pallas_call(functools.partial(exchange_kernel, rows), out_shape=jax.Sh...  21.4 us
    pallas_call x1, Pallas kernels, project(): pl.pallas_call(functools.partial(project_kernel, clusters), out_shape=[ja...  14.9 us
    pallas_call x1, Pallas kernels, spread_rows(): pl.pallas_call(pack_kernel, out_shape=jax.ShapeDtypeStruct((2 * rows * CA...  4.53 us
    pallas_call x1, Pallas kernels, new_basis(): pl.pallas_call(functools.partial(basis_kernel, last), out_shape=jax.Shape...  3.52 us

profile of v6, /device:TPU:0, one launch (start us, length us, event | category | flops | bytes accessed | tf_op | source)
XLA Modules:
  0.0 147.3 jit_solution(9997143488529069204)
XLA Ops:
  0.0 0.0 copy-start
  0.0 1.2 copy-done
  1.2 0.0 copy-start.2
  1.2 48.0 %covariance.4 = (bf16[1,32,16,512]{3,2,1,0:T(8,128)(2,1)S(1)}, bf16[3072,1024]{1,0:T(8,128)(2,1)S(1)}) custom-call(bf16[3072,1024]{1,0:T(8,128)(2,1)} %source.1, f32[1024,256]{1,0:T(8,128)S(1)} %copy-done), custom_call_target="tpu_custom_call" | custom-call | tf_op jit(solution)/shard_map/covariance/pallas_call | solution.py:349
  49.2 51.0 %covariance.5 = (bf16[1,32,16,512]{3,2,1,0:T(8,128)(2,1)S(1)}, f32[3,128,128]{2,1,0:T(8,128)S(1)}, f32[3,128,128]{2,1,0:T(8,128)S(1)}, f32[1,1]{1,0:T(1,128)}) custom-call(bf16[3072,1024]{1,0:T(8,128)(2,1)S(1)} %get-tuple-element.31.refs_0_, bf16[1,32,16,512]{3,2,1,0:T(8,128)(2,1)S(1)} %get-tuple-element.32.refs_1_), custom_call_target="tpu_custom_call" | custom-call | tf_op jit(solution)/shard_map/covariance/pallas_call | solution.py:349
  100.2 0.0 copy-start.1
  100.9 0.0 copy-done.2
  101.6 3.5 %new_basis.3.q = bf16[1024,256]{1,0:T(8,128)(2,1)S(1)} custom-call(s32[1]{0:T(128)S(6)} %copy.9.kept, f32[3,128,128]{2,1,0:T(8,128)S(1)} %get-tuple-element.37.gram, bf16[1,32,16,512]{3,2,1,0:T(8,128)(2,1)S(1)} %get-tuple-element.38.z), custom_call_target="tpu_custom_call" | custom-call | tf_op jit(solution)/shard_map/new_basis/pallas_call | solution.py:511
  105.1 0.0 copy-done.1
  105.2 14.9 %project.1 = (bf16[3072,128]{1,0:T(8,128)(2,1)S(1)}, s32[24,128]{1,0:T(8,128)S(1)}) custom-call(bf16[3072,1024]{1,0:T(8,128)(2,1)} %source.1, bf16[1024,256]{1,0:T(8,128)(2,1)S(1)} %new_basis.3.q, s32[24,128]{1,0:T(8,128)S(1)} %bitcast.5), custom_call_target="tpu_custom_call" | custom-call | tf_op jit(solution)/shard_map/project/pallas_call | solution.py:608
  120.1 4.5 %spread_rows.1.spread = f32[8192,128]{1,0:T(8,128)S(1)} custom-call(s32[3072]{0:T(1024)S(1)} %bitcast.6, s32[1]{0:T(128)} %bitcast.3.side, bf16[3072,128]{1,0:T(8,128)(2,1)S(1)} %get-tuple-element.40.p), custom_call_target="tpu_custom_call" | custom-call | tf_op jit(solution)/shard_map/spread_rows/pallas_call | solution.py:652
  124.6 21.4 %exchange.1.arrived = bf16[32,128,128]{2,1,0:T(8,128)(2,1)S(1)} custom-call(f32[8192,128]{1,0:T(8,128)S(1)} %spread_rows.1.spread), custom_call_target="tpu_custom_call" | custom-call | tf_op jit(solution)/shard_map/exchange/pallas_call | solution.py:695
  146.1 1.2 arrange.1
  (1 shorter events, 0.0 us)
Async XLA Ops:
  0.0 1.2 copy-start
  1.2 99.7 %copy-start.2 = (bf16[3072,1024]{1,0:T(8,128)(2,1)S(1)}, bf16[3072,1024]{1,0:T(8,128)(2,1)}, u32[]{:S(2)}) copy-start(bf16[3072,1024]{1,0:T(8,128)(2,1)} %source.1) | copy-start | bytes 18874372
  100.2 4.9 %copy-start.1 = (s32[3072,1]{0,1:T(1,128)S(1)}, s32[3072,1]{0,1:T(1,128)}, u32[]{:S(2)}) copy-start(s32[3072,1]{0,1:T(1,128)} %param.8) | copy-start | bytes 36868

commit v7 on v6

--- a/solution.py
+++ b/solution.py
@@ -519,7 +519,7 @@
     )(kept, gram, z)
 
 
-def project_kernel(clusters, source, q, ids, p_out, place, slab, away, home, keep, send, recv, p, near_sem, far_sem, p_sem, load_sem):
+def project_kernel(clusters, source, q, ids, doubled, place, slab, away, home, keep, send, recv, p, near_sem, far_sem, p_sem, load_sem):
     core, xl = lax.axis_index("core"), lax.axis_index("xl")
     near, far = {"core": 1 - core}, {"xl": 1 - xl}
     half_rows = slab.shape[0] // 2
@@ -586,16 +586,24 @@
             own.append(scores(1, i + 1))
         chip_sum(i, own[i])
     find_places(clusters, ids, place)
+
+    def double(own, i):
+        wide = p_at(own, i)[...].astype(F32)
+        low = lax.broadcasted_iota(jnp.int32, wide.shape, 1) < half // 2
+        turned = pltpu.roll(wide, half // 2, 1)
+        doubled[rows_at(own, i), :] = jnp.where(low == (core == 0), wide, turned)
+
     for i in range(count):
         to_far(i).wait_recv()
         p_at(1, i)[...] = (at(keep, i)[...] + at(recv, i)[...].astype(F32)).astype(BF16)
         share(i).start()
+        double(1, i)
     for i in range(count):
         to_near(i).wait_send()
         to_far(i).wait_send()
     for i in range(count):
         shared(i).wait_recv()
-    p_out[...] = p[...].reshape(p_out.shape)
+        double(0, i)
     for i in range(count):
         share(i).wait_send()
 
@@ -607,9 +615,12 @@
     dma = pltpu.SemaphoreType.DMA((2, len(SHARES)))
     return pl.pallas_call(
         functools.partial(project_kernel, clusters),
-        out_shape=[jax.ShapeDtypeStruct((length, half), BF16), jax.ShapeDtypeStruct(ids.shape, jnp.int32)],
+        out_shape=[
+            jax.ShapeDtypeStruct((length, half), F32),
+            jax.ShapeDtypeStruct(ids.shape, jnp.int32),
+        ],
         in_specs=[HBM, VMEM, VMEM],
-        out_specs=[VMEM, VMEM],
+        out_specs=[VMEM] * 2,
         scratch_shapes=[
             pltpu.VMEM(slab.shape, BF16),
             pltpu.VMEM((length // 2, width), BF16),
@@ -630,34 +641,26 @@
     )(slab, q, ids)
 
 
-def pack_kernel(place, side, p, spread, doubled):
-    length, lanes = p.shape
-    cols = lanes // 2
+def pack_kernel(place, doubled, spread):
     unroll = 16
-    low = lax.broadcasted_iota(jnp.int32, (length, lanes), 1) < cols
-    wide = p[...].astype(F32)
-    turned = pltpu.roll(wide, cols, 1)
-    doubled[...] = jnp.where(low == (side[0] == 0), wide, turned)
     spread[...] = jnp.zeros_like(spread)
 
-    @pl.loop(0, length // unroll)
+    @pl.loop(0, doubled.shape[0] // unroll)
     def _(step):
         for u in range(unroll):
             i = step * unroll + u
             spread[pl.ds(place[i], 1), :] = doubled[pl.ds(i, 1), :]
 
 
-def spread_rows(place, side, p, rows):
-    length, lanes = p.shape
+def spread_rows(place, doubled, slots):
     return pl.pallas_call(
         pack_kernel,
-        out_shape=jax.ShapeDtypeStruct((2 * rows * CAP, lanes), F32),
-        in_specs=[SMEM, SMEM, VMEM],
+        out_shape=jax.ShapeDtypeStruct((slots, doubled.shape[1]), F32),
+        in_specs=[SMEM, VMEM],
         out_specs=VMEM,
-        scratch_shapes=[pltpu.VMEM((length, lanes), F32)],
         compiler_params=pltpu.CompilerParams(vmem_limit_bytes=16 << 20),
         name="spread_rows",
-    )(place, side, p)
+    )(place, doubled)
 
 
 def exchange_kernel(rows, spread, out, buf, arrived, sem):
@@ -729,7 +732,6 @@
 
 
 def shards(rows, slab, basis, cluster_ids, kept):
-    side = jnp.broadcast_to(lax.axis_index("core"), (1,)).astype(jnp.int32)
     z, near_slab = covariance(slab, basis, rows, 0, True)
     for step in range(1, ITERS):
         after, gram, before, size = covariance(near_slab, z, rows, step)
@@ -742,8 +744,8 @@
 
         z, gram = lax.cond(size[0, 0] < TOL * TOL, kept_on, again, before, z, after, gram)
     q = new_basis(kept, gram, z, True)
-    p, place = project(slab, q, cluster_ids.reshape(-1, CAP), 2 * rows, ITERS)
-    spread = spread_rows(place.reshape(-1), side, p, rows)
+    doubled, place = project(slab, q, cluster_ids.reshape(-1, CAP), 2 * rows, ITERS)
+    spread = spread_rows(place.reshape(-1), doubled, 2 * rows * CAP)
     return jnp.swapaxes(arrange(exchange(spread, rows, ITERS + 1)), 1, 2)
 
 

time: 147 us -> 148 us (level)
  no operation moved by 1% of the time
where the time goes in v7:
time: 148 us; the launch traced here: 147 us
  Pallas kernels  144 us (97%)
    pallas_call x2, Pallas kernels, covariance(): pl.pallas_call(functools.partial(covariance_kernel, rows, kind), out_shap...  99 us
    pallas_call x1, Pallas kernels, exchange(): pl.pallas_call(functools.partial(exchange_kernel, rows), out_shape=jax.Sh...  21.5 us
    pallas_call x1, Pallas kernels, project(): pl.pallas_call(functools.partial(project_kernel, clusters), out_shape=[ja...  14.9 us
    pallas_call x1, Pallas kernels, spread_rows(): pl.pallas_call(pack_kernel, out_shape=jax.ShapeDtypeStruct((slots, double...  4.24 us
    pallas_call x1, Pallas kernels, new_basis(): pl.pallas_call(functools.partial(basis_kernel, last), out_shape=jax.Shape...  3.52 us

profile of v7, /device:TPU:0, one launch (start us, length us, event | category | flops | bytes accessed | tf_op | source)
XLA Modules:
  0.0 147.1 jit_solution(6210562329116858498)
XLA Ops:
  0.0 0.0 copy-start
  0.0 1.2 copy-done
  1.2 0.0 copy-start.2
  1.2 48.0 %covariance.4 = (bf16[1,32,16,512]{3,2,1,0:T(8,128)(2,1)S(1)}, bf16[3072,1024]{1,0:T(8,128)(2,1)S(1)}) custom-call(bf16[3072,1024]{1,0:T(8,128)(2,1)} %source.1, f32[1024,256]{1,0:T(8,128)S(1)} %copy-done), custom_call_target="tpu_custom_call" | custom-call | tf_op jit(solution)/shard_map/covariance/pallas_call | solution.py:349
  49.2 51.0 %covariance.5 = (bf16[1,32,16,512]{3,2,1,0:T(8,128)(2,1)S(1)}, f32[3,128,128]{2,1,0:T(8,128)S(1)}, f32[3,128,128]{2,1,0:T(8,128)S(1)}, f32[1,1]{1,0:T(1,128)}) custom-call(bf16[3072,1024]{1,0:T(8,128)(2,1)S(1)} %get-tuple-element.31.refs_0_, bf16[1,32,16,512]{3,2,1,0:T(8,128)(2,1)S(1)} %get-tuple-element.32.refs_1_), custom_call_target="tpu_custom_call" | custom-call | tf_op jit(solution)/shard_map/covariance/pallas_call | solution.py:349
  100.2 0.0 copy-start.1
  100.9 0.0 copy-done.2
  101.6 3.5 %new_basis.3.q = bf16[1024,256]{1,0:T(8,128)(2,1)S(1)} custom-call(s32[1]{0:T(128)S(6)} %copy.9.kept, f32[3,128,128]{2,1,0:T(8,128)S(1)} %get-tuple-element.37.gram, bf16[1,32,16,512]{3,2,1,0:T(8,128)(2,1)S(1)} %get-tuple-element.38.z), custom_call_target="tpu_custom_call" | custom-call | tf_op jit(solution)/shard_map/new_basis/pallas_call | solution.py:511
  105.1 0.0 copy-done.1
  105.2 14.9 %project.1 = (f32[3072,128]{1,0:T(8,128)S(1)}, s32[24,128]{1,0:T(8,128)S(1)}) custom-call(bf16[3072,1024]{1,0:T(8,128)(2,1)} %source.1, bf16[1024,256]{1,0:T(8,128)(2,1)S(1)} %new_basis.3.q, s32[24,128]{1,0:T(8,128)S(1)} %bitcast.4), custom_call_target="tpu_custom_call" | custom-call | tf_op jit(solution)/shard_map/project/pallas_call | solution.py:616
  120.1 4.2 %spread_rows.1.spread = f32[8192,128]{1,0:T(8,128)S(1)} custom-call(s32[3072]{0:T(1024)S(1)} %bitcast.5, f32[3072,128]{1,0:T(8,128)S(1)} %get-tuple-element.40.doubled), custom_call_target="tpu_custom_call" | custom-call | tf_op jit(solution)/shard_map/spread_rows/pallas_call | solution.py:656
  124.3 21.5 %exchange.1.arrived = bf16[32,128,128]{2,1,0:T(8,128)(2,1)S(1)} custom-call(f32[8192,128]{1,0:T(8,128)S(1)} %spread_rows.1.spread), custom_call_target="tpu_custom_call" | custom-call | tf_op jit(solution)/shard_map/exchange/pallas_call | solution.py:698
  145.9 1.2 arrange.1
  (1 shorter events, 0.0 us)
Async XLA Ops:
  0.0 1.2 copy-start
  1.2 99.7 %copy-start.2 = (bf16[3072,1024]{1,0:T(8,128)(2,1)S(1)}, bf16[3072,1024]{1,0:T(8,128)(2,1)}, u32[]{:S(2)}) copy-start(bf16[3072,1024]{1,0:T(8,128)(2,1)} %source.1) | copy-start | bytes 18874372
  100.2 4.9 %copy-start.1 = (s32[3072,1]{0,1:T(1,128)S(1)}, s32[3072,1]{0,1:T(1,128)}, u32[]{:S(2)}) copy-start(s32[3072,1]{0,1:T(1,128)} %param.8) | copy-start | bytes 36868

commit v8 on v7

--- a/solution.py
+++ b/solution.py
@@ -503,7 +503,7 @@
                 index = lax.broadcasted_iota(jnp.int32, (n, wide), 0)
                 qt = jnp.where(index < kept[0], qt, 0.0)
             left = (f * ns + s) * wide
-            q_out[left:left + wide, :] = qt.T.astype(BF16)
+            q_out[left:left + wide, :] = qt.astype(BF16).T
 
 
 def new_basis(kept, gram, z, last):
@@ -674,7 +674,7 @@
         start = pl.multiple_of(r * CAP, CAP)
         low = spread[pl.ds(start, CAP), :]
         high = spread[pl.ds(pl.multiple_of(start + rows * CAP, CAP), CAP), :]
-        return jnp.where(even, low, high).T.astype(BF16)
+        return jnp.where(even, low, high).astype(BF16).T
 
     def send(slot, there, at):
         return remote(buf.at[slot], arrived.at[at], sem.at[0, slot], sem.at[1, slot], {"rows": there})

time: 148 us -> 147 us (level)
  no operation moved by 1% of the time
where the time goes in v8:
time: 147 us
  Pallas kernels  144 us (98%)
    pallas_call x2, Pallas kernels, covariance(): pl.pallas_call(functools.partial(covariance_kernel, rows, kind), out_shap...  99 us
    pallas_call x1, Pallas kernels, exchange(): pl.pallas_call(functools.partial(exchange_kernel, rows), out_shape=jax.Sh...  21.6 us
    pallas_call x1, Pallas kernels, project(): pl.pallas_call(functools.partial(project_kernel, clusters), out_shape=[ja...  14.9 us
    pallas_call x1, Pallas kernels, spread_rows(): pl.pallas_call(pack_kernel, out_shape=jax.ShapeDtypeStruct((slots, double...  4.24 us
    pallas_call x1, Pallas kernels, new_basis(): pl.pallas_call(functools.partial(basis_kernel, last), out_shape=jax.Shape...  3.52 us

profile of v8, /device:TPU:0, one launch (start us, length us, event | category | flops | bytes accessed | tf_op | source)
XLA Modules:
  0.0 147.1 jit_solution(11862029126216587316)
XLA Ops:
  0.0 0.0 copy-start
  0.0 1.2 copy-done
  1.2 0.0 copy-start.2
  1.2 48.0 %covariance.4 = (bf16[1,32,16,512]{3,2,1,0:T(8,128)(2,1)S(1)}, bf16[3072,1024]{1,0:T(8,128)(2,1)S(1)}) custom-call(bf16[3072,1024]{1,0:T(8,128)(2,1)} %source.1, f32[1024,256]{1,0:T(8,128)S(1)} %copy-done), custom_call_target="tpu_custom_call" | custom-call | tf_op jit(solution)/shard_map/covariance/pallas_call | solution.py:349
  49.2 51.0 %covariance.5 = (bf16[1,32,16,512]{3,2,1,0:T(8,128)(2,1)S(1)}, f32[3,128,128]{2,1,0:T(8,128)S(1)}, f32[3,128,128]{2,1,0:T(8,128)S(1)}, f32[1,1]{1,0:T(1,128)}) custom-call(bf16[3072,1024]{1,0:T(8,128)(2,1)S(1)} %get-tuple-element.31.refs_0_, bf16[1,32,16,512]{3,2,1,0:T(8,128)(2,1)S(1)} %get-tuple-element.32.refs_1_), custom_call_target="tpu_custom_call" | custom-call | tf_op jit(solution)/shard_map/covariance/pallas_call | solution.py:349
  100.2 0.0 copy-start.1
  100.9 0.0 copy-done.2
  101.6 3.5 %new_basis.3.q = bf16[1024,256]{1,0:T(8,128)(2,1)S(1)} custom-call(s32[1]{0:T(128)S(6)} %copy.9.kept, f32[3,128,128]{2,1,0:T(8,128)S(1)} %get-tuple-element.37.gram, bf16[1,32,16,512]{3,2,1,0:T(8,128)(2,1)S(1)} %get-tuple-element.38.z), custom_call_target="tpu_custom_call" | custom-call | tf_op jit(solution)/shard_map/new_basis/pallas_call | solution.py:511
  105.1 0.0 copy-done.1
  105.2 14.9 %project.1 = (f32[3072,128]{1,0:T(8,128)S(1)}, s32[24,128]{1,0:T(8,128)S(1)}) custom-call(bf16[3072,1024]{1,0:T(8,128)(2,1)} %source.1, bf16[1024,256]{1,0:T(8,128)(2,1)S(1)} %new_basis.3.q, s32[24,128]{1,0:T(8,128)S(1)} %bitcast.4), custom_call_target="tpu_custom_call" | custom-call | tf_op jit(solution)/shard_map/project/pallas_call | solution.py:616
  120.1 4.2 %spread_rows.1.spread = f32[8192,128]{1,0:T(8,128)S(1)} custom-call(s32[3072]{0:T(1024)S(1)} %bitcast.5, f32[3072,128]{1,0:T(8,128)S(1)} %get-tuple-element.40.doubled), custom_call_target="tpu_custom_call" | custom-call | tf_op jit(solution)/shard_map/spread_rows/pallas_call | solution.py:656
  124.3 21.6 %exchange.1.arrived = bf16[32,128,128]{2,1,0:T(8,128)(2,1)S(1)} custom-call(f32[8192,128]{1,0:T(8,128)S(1)} %spread_rows.1.spread), custom_call_target="tpu_custom_call" | custom-call | tf_op jit(solution)/shard_map/exchange/pallas_call | solution.py:698
  145.9 1.2 arrange.1
  (1 shorter events, 0.0 us)
Async XLA Ops:
  0.0 1.2 copy-start
  1.2 99.7 %copy-start.2 = (bf16[3072,1024]{1,0:T(8,128)(2,1)S(1)}, bf16[3072,1024]{1,0:T(8,128)(2,1)}, u32[]{:S(2)}) copy-start(bf16[3072,1024]{1,0:T(8,128)(2,1)} %source.1) | copy-start | bytes 18874372
  100.2 4.9 %copy-start.1 = (s32[3072,1]{0,1:T(1,128)S(1)}, s32[3072,1]{0,1:T(1,128)}, u32[]{:S(2)}) copy-start(s32[3072,1]{0,1:T(1,128)} %param.8) | copy-start | bytes 36868

commit v9 on v8

--- a/solution.py
+++ b/solution.py
@@ -13,8 +13,8 @@
 SHARES = (1, 2, 2, 2, 2, 2, 1)
 NS = 1
 GRANT = 44
-TOL = 2e-3
-COARSE = 1.0
+TOL = 4e-3
+COARSE = 0.5
 STEPS = 14
 F32 = jnp.float32
 BF16 = jnp.bfloat16

time: 147 us -> 148 us (level)
  no operation moved by 1% of the time
where the time goes in v9:
time: 148 us
  Pallas kernels  145 us (98%)
    pallas_call x2, Pallas kernels, covariance(): pl.pallas_call(functools.partial(covariance_kernel, rows, kind), out_shap...  99 us
    pallas_call x1, Pallas kernels, exchange(): pl.pallas_call(functools.partial(exchange_kernel, rows), out_shape=jax.Sh...  21.5 us
    pallas_call x1, Pallas kernels, project(): pl.pallas_call(functools.partial(project_kernel, clusters), out_shape=[ja...  14.9 us
    pallas_call x1, Pallas kernels, spread_rows(): pl.pallas_call(pack_kernel, out_shape=jax.ShapeDtypeStruct((slots, double...  4.24 us
    pallas_call x1, Pallas kernels, new_basis(): pl.pallas_call(functools.partial(basis_kernel, last), out_shape=jax.Shape...  4.06 us

profile of v9, /device:TPU:0, one launch (start us, length us, event | category | flops | bytes accessed | tf_op | source)
XLA Modules:
  0.0 147.6 jit_solution(13396691598408487353)
XLA Ops:
  0.0 0.0 copy-start
  0.0 1.2 copy-done
  1.2 0.0 copy-start.2
  1.2 48.0 %covariance.4 = (bf16[1,32,16,512]{3,2,1,0:T(8,128)(2,1)S(1)}, bf16[3072,1024]{1,0:T(8,128)(2,1)S(1)}) custom-call(bf16[3072,1024]{1,0:T(8,128)(2,1)} %source.1, f32[1024,256]{1,0:T(8,128)S(1)} %copy-done), custom_call_target="tpu_custom_call" | custom-call | tf_op jit(solution)/shard_map/covariance/pallas_call | solution.py:349
  49.2 51.0 %covariance.5 = (bf16[1,32,16,512]{3,2,1,0:T(8,128)(2,1)S(1)}, f32[3,128,128]{2,1,0:T(8,128)S(1)}, f32[3,128,128]{2,1,0:T(8,128)S(1)}, f32[1,1]{1,0:T(1,128)}) custom-call(bf16[3072,1024]{1,0:T(8,128)(2,1)S(1)} %get-tuple-element.31.refs_0_, bf16[1,32,16,512]{3,2,1,0:T(8,128)(2,1)S(1)} %get-tuple-element.32.refs_1_), custom_call_target="tpu_custom_call" | custom-call | tf_op jit(solution)/shard_map/covariance/pallas_call | solution.py:349
  100.2 0.0 copy-start.1
  100.9 0.0 copy-done.2
  101.6 4.1 %new_basis.3.q = bf16[1024,256]{1,0:T(8,128)(2,1)S(1)} custom-call(s32[1]{0:T(128)S(6)} %copy.9.kept, f32[3,128,128]{2,1,0:T(8,128)S(1)} %get-tuple-element.37.gram, bf16[1,32,16,512]{3,2,1,0:T(8,128)(2,1)S(1)} %get-tuple-element.38.z), custom_call_target="tpu_custom_call" | custom-call | tf_op jit(solution)/shard_map/new_basis/pallas_call | solution.py:511
  105.7 0.0 copy-done.1
  105.7 14.9 %project.1 = (f32[3072,128]{1,0:T(8,128)S(1)}, s32[24,128]{1,0:T(8,128)S(1)}) custom-call(bf16[3072,1024]{1,0:T(8,128)(2,1)} %source.1, bf16[1024,256]{1,0:T(8,128)(2,1)S(1)} %new_basis.3.q, s32[24,128]{1,0:T(8,128)S(1)} %bitcast.4), custom_call_target="tpu_custom_call" | custom-call | tf_op jit(solution)/shard_map/project/pallas_call | solution.py:616
  120.6 4.2 %spread_rows.1.spread = f32[8192,128]{1,0:T(8,128)S(1)} custom-call(s32[3072]{0:T(1024)S(1)} %bitcast.5, f32[3072,128]{1,0:T(8,128)S(1)} %get-tuple-element.40.doubled), custom_call_target="tpu_custom_call" | custom-call | tf_op jit(solution)/shard_map/spread_rows/pallas_call | solution.py:656
  124.9 21.5 %exchange.1.arrived = bf16[32,128,128]{2,1,0:T(8,128)(2,1)S(1)} custom-call(f32[8192,128]{1,0:T(8,128)S(1)} %spread_rows.1.spread), custom_call_target="tpu_custom_call" | custom-call | tf_op jit(solution)/shard_map/exchange/pallas_call | solution.py:698
  146.4 1.2 arrange.1
  (1 shorter events, 0.0 us)
Async XLA Ops:
  0.0 1.2 copy-start
  1.2 99.7 %copy-start.2 = (bf16[3072,1024]{1,0:T(8,128)(2,1)S(1)}, bf16[3072,1024]{1,0:T(8,128)(2,1)}, u32[]{:S(2)}) copy-start(bf16[3072,1024]{1,0:T(8,128)(2,1)} %source.1) | copy-start | bytes 18874372
  100.2 5.5 %copy-start.1 = (s32[3072,1]{0,1:T(1,128)S(1)}, s32[3072,1]{0,1:T(1,128)}, u32[]{:S(2)}) copy-start(s32[3072,1]{0,1:T(1,128)} %param.8) | copy-start | bytes 36868
